TPU v7x, 128 devices: a whole 4x4x4 slice. The times are simulated.
128 devices in a mesh: gx: 4 (over x), gy: 32 (over z, y, core).
Axes of the slice: x: 4, y: 4, z: 4, core: 2. Of those that a mesh axis runs over, the one named last changes fastest.
Arguments:
- particles: bfloat16 [131072, 128], P(('gx', 'gy')), may hold values from -6 to 6
- weights: bfloat16 [131072], P(('gx', 'gy')), may hold values from 0.099609375 to 1
- detections: bfloat16 [65536, 128], P(('gx', 'gy')), may hold values from -6 to 6
- clutter: float32 [65536], P(('gx', 'gy')), may hold values from 4096 to 40960
- gate_ids: int32 [1024, 16], P(('gx', 'gy')), may hold values from 0 to 127, all different within a row; in each aligned block of 8 rows (0 to 7, 8 to 15, ...) at most 2 rows name the same one
- gate_lens: int32 [1024], P(('gx', 'gy')), may hold values from 10 to 16
Outputs:
- updated: float32 [131072], P(('gx', 'gy'))
- log_norm: float32 [65536], P(('gx', 'gy'))
- estimate: float32 [65536, 128], P(('gx', 'gy'))
Inputs may be any that keep to these rules, and one draw needn't show every extreme that they name: `gate_ids`: each row names 16 different detection blocks, of which only the first gate_lens entries are used. Over the 8 rows of one device no detection block is named more than 2 times, and some device names some block exactly 2 times.
All inputs are finite; a program needn't handle non-finite values.
Results may differ from a plain program's by a relative error of at most 0.00084.
Values may be sent and summed in bfloat16 or wider, within the bound.
No kernel may reach another device: no remote copies, remote signals or barrier semaphores. Data moves between devices by JAX's collectives and lax.ppermute only.
A program may use at most 64 MiB of HBM per device.

v0:
```python
import math

import jax
import jax.numpy as jnp
from jax import lax
from jax.sharding import PartitionSpec as P

PBS = 128


DETECT_PROB = 0.9
SPREAD = 8.0


def slot_plan(gate_ids, gate_lens, peer_count, capacity):
    own_blocks, listed = gate_ids.shape
    flat_ids = gate_ids.reshape(-1)
    active = (jnp.arange(listed, dtype=jnp.int32)[None, :] < gate_lens[:, None]).reshape(-1)
    onehot = (
        (flat_ids[:, None] == jnp.arange(peer_count, dtype=jnp.int32)[None, :]) & active[:, None]
    ).astype(jnp.int32)
    before = jnp.cumsum(onehot, axis=0) - onehot
    ranking = jnp.sum(before * onehot, axis=1)
    slots_at = jnp.where(active, flat_ids * capacity + ranking, peer_count * capacity)
    owner_block = jnp.repeat(jnp.arange(own_blocks, dtype=jnp.int32), listed)
    source = (
        jnp.full((peer_count * capacity,), own_blocks, jnp.int32)
        .at[slots_at]
        .set(owner_block, mode="drop")
    )
    return (active, slots_at, source)


def local(particles, weights, detections, clutter, gate_ids, gate_lens):
    peer_count = lax.axis_size(("gx", "gy"))
    own_blocks, listed = gate_ids.shape
    features = particles.shape[1]
    capacity = max(2, 2 * own_blocks * listed // peer_count)
    slot_total = peer_count * capacity
    offset = features / 8.0
    active, slots_at, source = slot_plan(gate_ids, gate_lens, peer_count, capacity)
    valid = source < own_blocks
    chosen = jnp.minimum(source, own_blocks - 1)
    grouped = particles.reshape(own_blocks, PBS, features)
    outgoing = jnp.where(valid[:, None, None], grouped[chosen], jnp.zeros((), jnp.bfloat16))
    out_weights = jnp.where(
        valid[:, None], weights.reshape(own_blocks, PBS)[chosen], jnp.zeros((), jnp.bfloat16)
    )
    outgoing = outgoing.reshape(peer_count, capacity, PBS, features)
    out_weights = out_weights.reshape(peer_count, capacity, PBS)
    arrived, arrived_weights = (
        lax.all_to_all(outgoing, ("gx", "gy"), split_axis=0, concat_axis=0, tiled=True),
        lax.all_to_all(out_weights, ("gx", "gy"), split_axis=0, concat_axis=0, tiled=True),
    )
    group_size = math.gcd(slot_total, max(1, 2048 // PBS))
    steps_count = slot_total // group_size
    stacked = arrived.reshape(steps_count, group_size * PBS, features)
    stacked_weights = arrived_weights.reshape(steps_count, group_size * PBS)
    det_half = 0.5 * jnp.sum(jnp.square(detections.astype(jnp.float32)), axis=1)

    def likelihood(block_rows, rows_half):
        cross_term = jnp.einsum(
            "rf,df->rd", block_rows, detections, preferred_element_type=jnp.float32
        )
        return jnp.exp((cross_term - rows_half[:, None] - det_half[None, :]) / SPREAD + offset)

    def first_pass(running, inputs):
        mass_sum, moment = running
        block_rows, block_weights = inputs
        rows_half = 0.5 * jnp.sum(jnp.square(block_rows.astype(jnp.float32)), axis=1)
        weighted = likelihood(block_rows, rows_half) * block_weights.astype(jnp.float32)[:, None]
        mass_sum = mass_sum + jnp.sum(weighted, axis=0)
        moment = moment + jnp.einsum(
            "rd,rf->df",
            weighted.astype(jnp.bfloat16),
            block_rows,
            preferred_element_type=jnp.float32,
        )
        return ((mass_sum, moment), rows_half)

    start_state = (
        jnp.zeros((detections.shape[0],), jnp.float32),
        jnp.zeros((detections.shape[0], features), jnp.float32),
    )
    (mass_sum, moment), halves = lax.scan(first_pass, start_state, (stacked, stacked_weights))
    normalizer = clutter + DETECT_PROB * mass_sum
    log_norm = jnp.log(normalizer)
    estimate = DETECT_PROB * moment / normalizer[:, None]
    inverse_low = (1.0 / normalizer).astype(jnp.bfloat16)

    def second_pass(running, inputs):
        block_rows, rows_half = inputs
        likelihood_low = likelihood(block_rows, rows_half).astype(jnp.bfloat16)
        return (running, jnp.dot(likelihood_low, inverse_low, preferred_element_type=jnp.float32))

    unused, partial_value = lax.scan(second_pass, jnp.zeros((), jnp.float32), (stacked, halves))
    returned = lax.all_to_all(
        partial_value.reshape(peer_count, capacity, PBS),
        ("gx", "gy"),
        split_axis=0,
        concat_axis=0,
        tiled=True,
    )
    returned = returned.reshape(slot_total, PBS)
    fetched = jnp.where(active[:, None], returned[jnp.minimum(slots_at, slot_total - 1)], 0.0)
    summed = jnp.sum(fetched.reshape(own_blocks, listed, PBS), axis=1)
    factor = 1.0 - DETECT_PROB + DETECT_PROB * summed.reshape(-1)
    updated = weights.astype(jnp.float32) * factor
    return (updated, log_norm, estimate)


def solution(mesh):
    return jax.shard_map(
        local,
        mesh=mesh,
        in_specs=(
            P(("gx", "gy"), None),
            P(("gx", "gy")),
            P(("gx", "gy"), None),
            P(("gx", "gy")),
            P(("gx", "gy"), None),
            P(("gx", "gy")),
        ),
        out_specs=(P(("gx", "gy")), P(("gx", "gy")), P(("gx", "gy"), None)),
        check_vma=False,
    )
```

profile of v0, /device:TPU:0, one launch (start us, length us, event | category | flops | bytes accessed | tf_op | source)
XLA Modules:
  0.0 306.4 jit_solution(731377531376333923)
XLA Ops:
  7.1 11.1 %all-to-all-start.1 = ((bf16[128,2,128]{2,1,0:T(2,128)(2,1)}), bf16[128,2,128]{2,1,0:T(2,128)(2,1)S(1)}, u32[]{:S(2)}, u32[]{:S(2)}) async-start(bf16[128,2,128]{2,1,0:T(2,128)(2,1)} %broadcast_select_fusion.1), calls=%async_computation.1 | async-start | bytes 131072 | tf_op jit(solution)/shard_map/all_to_all | solution.py:53
  18.3 8.4 %gather_fusion = bf16[256,128,128]{2,1,0:T(8,128)(2,1)} fusion(bf16[8,128,128]{2,1,0:T(8,128)(2,1)S(1)} %bitcast.64, s32[1024]{0:T(1024)S(1)} %pad_clamp_fusion.1), kind=kCustom, calls=%fused_computation | custom fusion | bytes 16778240 | tf_op jit(solution)/shard_map/gather | solution.py:45
  26.6 7.3 %broadcast_select_fusion = bf16[128,2,128,128]{3,2,1,0:T(8,128)(2,1)} fusion(bf16[128,2,128,128]{3,2,1,0:T(8,128)(2,1)} %bitcast.66, pred[128,2]{1,0:T(8,128)(4,1)S(1)} %broadcast_in_dim.79), kind=kLoop, calls=%fused_computation.26 | loop fusion | flops 4194304 | bytes 16777472 | tf_op jit(solution)/shard_map/jit(_where)/select_n | solution.py:45
  33.9 10.3 %all-to-all-start = ((bf16[128,2,128,128]{3,2,1,0:T(8,128)(2,1)}), bf16[128,2,128,128]{3,2,1,0:T(8,128)(2,1)}, u32[]{:S(2)}, u32[]{:S(2)}) async-start(bf16[128,2,128,128]{3,2,1,0:T(8,128)(2,1)} %broadcast_select_fusion), calls=%async_computation | async-start | bytes 16777216 | tf_op jit(solution)/shard_map/all_to_all | solution.py:52
  44.5 105.9 %all-to-all-done = bf16[128,2,128,128]{3,2,1,0:T(8,128)(2,1)} async-done(((bf16[128,2,128,128]{3,2,1,0:T(8,128)(2,1)}), bf16[128,2,128,128]{3,2,1,0:T(8,128)(2,1)}, u32[]{:S(2)}, u32[]{:S(2)}) %all-to-all-start) | async-done | bytes 8388640 | tf_op jit(solution)/shard_map/all_to_all | solution.py:52
  150.4 94.6 %while.26 = (s32[]{:T(128)}, f32[512]{0:T(512)S(1)}, f32[512,128]{1,0:T(8,128)S(1)}, f32[16,2048]{1,0:T(8,128)S(1)}, bf16[16,2048,128]{2,1,0:T(8,128)(2,1)}, /*i...) while((s32[]{:T(128)}, f32[512]{0:T(512)S(1)}, ...), condition=%wide.region_7.8_spmd.clone, body=%wide.region_4.7_spmd.clone.sunk | while | flops 545131008 | bytes 6503548 | solution.py:85
  151.9 2.4 fusion.49
  157.8 2.4 fusion.49
  163.7 2.4 fusion.49
  169.6 2.4 fusion.49
  175.5 2.4 fusion.49
  181.4 2.4 fusion.49
  187.3 2.4 fusion.49
  193.2 2.4 fusion.49
  199.2 2.4 fusion.49
  205.1 2.4 fusion.49
  211.0 2.4 fusion.49
  216.9 2.4 fusion.49
  228.7 2.4 fusion.49
  234.6 2.4 fusion.49
  240.5 2.4 fusion.49
  245.6 41.2 %while.25 = (s32[]{:T(128)}, f32[16,2048]{1,0:T(8,128)S(1)}, bf16[16,2048,128]{2,1,0:T(8,128)(2,1)}, bf16[512,128]{1,0:T(8,128)(2,1)S(1)}, f32[16,2048]{1,0:T(8,...) while((s32[]{:T(128)}, f32[16,2048]{1,0:T(8,128)S(1)}, ...), condition=%wide.region_9.10_spmd, body=%wide.region_8.9_spmd.sunk | while | flops 275775488 | bytes 710245 | solution.py:96
  287.6 8.0 %all-to-all-start.2 = ((f32[128,2,128]{2,1,0:T(2,128)}), f32[128,2,128]{2,1,0:T(2,128)S(1)}, u32[]{:S(2)}, u32[]{:S(2)}) async-start(f32[128,2,128]{2,1,0:T(2,128)} %reshape.175), calls=%async_computation.2 | async-start | bytes 262144 | tf_op jit(solution)/shard_map/all_to_all | solution.py:97
  296.5 8.6 %all-to-all-done.2 = f32[128,2,128]{2,1,0:T(2,128)S(1)} async-done(((f32[128,2,128]{2,1,0:T(2,128)}), f32[128,2,128]{2,1,0:T(2,128)S(1)}, u32[]{:S(2)}, u32[]{:S(2)}) %all-to-all-start.2) | async-done | bytes 131104 | tf_op jit(solution)/shard_map/all_to_all | solution.py:97
  (204 shorter events, 108.4 us)
Async XLA Ops:
  0.6 17.6 %copy-start = (bf16[1024,128]{1,0:T(8,128)(2,1)S(1)}, bf16[1024,128]{1,0:T(8,128)(2,1)}, u32[]{:S(2)}) copy-start(bf16[1024,128]{1,0:T(8,128)(2,1)} %param.10) | copy-start | bytes 786436
  7.1 26.8 %all-to-all-start.1 = ((bf16[128,2,128]{2,1,0:T(2,128)(2,1)}), bf16[128,2,128]{2,1,0:T(2,128)(2,1)S(1)}, u32[]{:S(2)}, u32[]{:S(2)}) async-start(bf16[128,2,128]{2,1,0:T(2,128)(2,1)} %broadcast_select_fusion.1), calls=%async_computation.1 | async-start | bytes 131072 | tf_op jit(solution)/shard_map/all_to_all | solution.py:53
  33.9 10.4 %copy-start.2 = (bf16[512,128]{1,0:T(8,128)(2,1)S(1)}, bf16[512,128]{1,0:T(8,128)(2,1)}, u32[]{:S(2)}) copy-start(bf16[512,128]{1,0:T(8,128)(2,1)} %param.12) | copy-start | bytes 393220
  33.9 116.5 %all-to-all-start = ((bf16[128,2,128,128]{3,2,1,0:T(8,128)(2,1)}), bf16[128,2,128,128]{3,2,1,0:T(8,128)(2,1)}, u32[]{:S(2)}, u32[]{:S(2)}) async-start(bf16[128,2,128,128]{3,2,1,0:T(8,128)(2,1)} %broadcast_select_fusion), calls=%async_computation | async-start | bytes 16777216 | tf_op jit(solution)/shard_map/all_to_all | solution.py:52
  150.4 94.6 %copy-start.3 = (f32[512]{0:T(512)S(1)}, f32[512]{0:T(512)}, u32[]{:S(2)}) copy-start(f32[512]{0:T(512)} %param.13) | copy-start | bytes 6148
  245.6 60.2 %copy-start.1 = (bf16[1024]{0:T(1024)(128)(2,1)S(1)}, bf16[1024]{0:T(1024)(128)(2,1)}, u32[]{:S(2)}) copy-start(bf16[1024]{0:T(1024)(128)(2,1)} %param.11) | copy-start | bytes 6148
  287.6 17.4 %all-to-all-start.2 = ((f32[128,2,128]{2,1,0:T(2,128)}), f32[128,2,128]{2,1,0:T(2,128)S(1)}, u32[]{:S(2)}, u32[]{:S(2)}) async-start(f32[128,2,128]{2,1,0:T(2,128)} %reshape.175), calls=%async_computation.2 | async-start | bytes 262144 | tf_op jit(solution)/shard_map/all_to_all | solution.py:97
where the time goes:
time: 311 us; the launch traced here: 306 us
  waiting for transfers between devices  114 us (37%)
  matrix products  105 us (34%)
  other arithmetic  35.1 us (11%)
  starting transfers between devices  29.5 us (9%)
  local copies, waits for them, and re-layouts  20 us (6%)
    all_to_all x1, waiting for transfers between devices, local(): lax.all_to_all(outgoing, ('gx', 'gy'), split_axis=0, concat_axis=0, tiled...  106 us
    dot_general x16, matrix products, likelihood(): jnp.einsum('rf,df->rd', block_rows, detections, preferred_element_type=jn...  38.3 us
    dot_general x16, matrix products, second_pass(): jnp.dot(likelihood_low, inverse_low, preferred_element_type=jnp.float32)  37.4 us
    dot_general x16, matrix products, first_pass(): jnp.einsum('rd,rf->df', weighted.astype(jnp.bfloat16), block_rows, prefer...  29.2 us
    reduce_sum x16, other arithmetic, first_pass(): jnp.sum(jnp.square(block_rows.astype(jnp.float32)), axis=1)  22.2 us
    all_to_all x1, starting transfers between devices, local(): lax.all_to_all(out_weights, ('gx', 'gy'), split_axis=0, concat_axis=0, ti...  11.1 us
    all_to_all x1, starting transfers between devices, local(): lax.all_to_all(outgoing, ('gx', 'gy'), split_axis=0, concat_axis=0, tiled...  10.3 us
    all_to_all x1, waiting for transfers between devices, local(): lax.all_to_all(partial_value.reshape(peer_count, capacity, PBS), ('gx', '...  8.56 us
  transfers between devices with their start and end apart: 3, of which 2 were waited for; matrix products, arithmetic and copies ran while one was open for 5% of the time, Pallas kernels for 0%

commit v1 on v0

v1 whole, which is shorter than its diff:
```python
import jax
import jax.numpy as jnp
from jax import lax
from jax.experimental import pallas as pl
from jax.experimental.pallas import tpu as pltpu
from jax.sharding import PartitionSpec as P

PBS = 128
DBS = 512
DETECT_PROB = 0.9
LOG2E = 1.4426950408889634
SCALE = LOG2E / 8.0
BLOCKS = 128
SLOTS = 136
META = 1024
ROWS = 1072

f32 = jnp.float32
bf16 = jnp.bfloat16


def alpha_groups():
    return [[a * 2 + c for a in range(16)] for c in range(2)]


def core_swap(v):
    return lax.ppermute(v, "gy", [(i, i ^ 1) for i in range(32)])


def x_shift(v, s):
    return lax.ppermute(v, "gx", [(i, (i + s) % 4) for i in range(4)])


def pair_kernel(mask_ref, pos_ref, recv_ref, det_ref, as_ref, mom_ref, mass_ref, low_ref, slot_ref,
                lst, wrow, brow, buf, sem):
    x, c = pos_ref[0], pos_ref[1]
    for s in range(16):
        wb = recv_ref[s, META:META + 16, :].astype(f32)
        ml = recv_ref[s, META + 16:META + 32, :].astype(f32)
        wrow[s * 8:(s + 1) * 8, :] = wb[:8]
        brow[s * 8:(s + 1) * 8, :] = wb[8:] + ml[:8] + ml[8:]
    wrow[BLOCKS:BLOCKS + 8, :] = jnp.zeros((8, 128), f32)
    mom_ref[...] = jnp.zeros_like(mom_ref)
    mass_ref[...] = jnp.zeros_like(mass_ref)

    bits = [((x + 4 - r // 2) % 4) * 2 + (c ^ (r % 2)) for r in range(8)]

    def scan_block(b, counts):
        m = mask_ref[b]
        out = []
        for r in range(8):
            lst[r, counts[r]] = b
            out.append(counts[r] + ((m >> bits[r]) & 1))
        return tuple(out)

    counts = lax.fori_loop(0, BLOCKS, scan_block, tuple(jnp.int32(0) for _ in range(8)))
    q = jnp.int32(0)
    for r in range(8):
        cnt = counts[r]

        def fill(p, q, r=r, cnt=cnt):
            slot_ref[0, q] = lst[r, 2 * p]
            slot_ref[1, q] = jnp.where(2 * p + 1 < cnt, lst[r, 2 * p + 1], BLOCKS)
            slot_ref[2, q] = r
            return q + 1

        q = lax.fori_loop(0, (cnt + 1) // 2, fill, q)
    slot_ref[3, 0] = q
    n = q

    def copy_out(q, s):
        return pltpu.make_async_copy(buf.at[s], low_ref.at[q], sem.at[s])

    def step(q, carry):
        b0, b1, r = slot_ref[0, q], slot_ref[1, q], slot_ref[2, q]
        b1c = jnp.minimum(b1, BLOCKS - 1)
        x2 = jnp.concatenate(
            [recv_ref[b0 // 8, pl.ds((b0 % 8) * PBS, PBS), :], recv_ref[b1c // 8, pl.ds((b1c % 8) * PBS, PBS), :]],
            axis=0,
        )
        w2 = jnp.concatenate([wrow[pl.ds(b0, 1), :], wrow[pl.ds(b1, 1), :]], axis=1)
        s2 = jnp.concatenate([brow[pl.ds(b0, 1), :], brow[pl.ds(b1c, 1), :]], axis=1)
        slot = q & 1

        @pl.when(q >= 2)
        def _():
            copy_out(q - 2, slot).wait()

        half = DBS // 2
        for h in range(2):
            rows = slice(h * half, (h + 1) * half)
            cross = lax.dot_general(det_ref[r, rows, :], x2, (((1,), (1,)), ((), ())), preferred_element_type=f32)
            a = as_ref[r, rows, :]
            lik = jnp.exp2(cross * SCALE + (jnp.concatenate([a, a], axis=1) + s2))
            buf[slot, rows, :] = lik.astype(bf16)
            wtd = lik * w2
            mass_ref[r, rows, :] += wtd[:, :128] + wtd[:, 128:]
            mom_ref[r, rows, :] += jnp.dot(wtd.astype(bf16), x2, preferred_element_type=f32)
        copy_out(q, slot).start()
        return carry

    lax.fori_loop(0, n, step, 0)

    @pl.when(n >= 2)
    def _():
        copy_out(n - 2, n & 1).wait()

    @pl.when(n >= 1)
    def _():
        copy_out(n - 1, (n - 1) & 1).wait()


def share_kernel(slot_ref, inv_ref, low_ref, share_ref, buf, sem):
    share_ref[...] = jnp.zeros_like(share_ref)
    n = slot_ref[3, 0]
    depth = buf.shape[0]

    def copy_in(q, s):
        return pltpu.make_async_copy(low_ref.at[q], buf.at[s], sem.at[s])

    for d in range(depth):
        @pl.when(d < n)
        def _(d=d):
            copy_in(d, d).start()

    def step(q, carry):
        s = q % depth
        copy_in(q, s).wait()
        b0, b1, r = slot_ref[0, q], slot_ref[1, q], slot_ref[2, q]
        v = inv_ref[r]
        low = buf[s].astype(f32)
        t = jnp.sum(low * jnp.concatenate([v, v], axis=1), axis=0, keepdims=True)
        share_ref[pl.ds(b0, 1), :] += t[:, :128]
        share_ref[pl.ds(b1, 1), :] += t[:, 128:]

        @pl.when(q + depth < n)
        def _():
            copy_in(q + depth, s).start()

        return carry

    lax.fori_loop(0, n, step, 0)


def local(particles, weights, detections, clutter, gate_ids, gate_lens):
    gx, gy = lax.axis_index("gx"), lax.axis_index("gy")
    c, alpha = gy % 2, gy // 2

    two = jnp.stack([detections, core_swap(detections)])
    dets = jnp.concatenate([two] + [x_shift(two, s) for s in (1, 2, 3)])

    half = jnp.sum(jnp.square(particles.astype(f32)), axis=1).reshape(8, PBS) * (-0.5 * SCALE)
    hi = lax.reduce_precision(half, 8, 7)
    mid = lax.reduce_precision(half - hi, 8, 7)
    lo = (half - hi) - mid
    live = jnp.arange(16, dtype=jnp.int32)[None, :] < gate_lens[:, None]
    bit = jnp.where(live, 1 << ((gate_ids // 32) * 2 + gate_ids % 2), 0)
    home = (gate_ids % 32) // 2
    masks = jnp.sum(jnp.where(home[:, :, None] == jnp.arange(16)[None, None, :], bit[:, :, None], 0), axis=1)
    payload = jnp.concatenate(
        [
            particles,
            weights.reshape(8, PBS),
            hi.astype(bf16),
            mid.astype(bf16),
            lo.astype(bf16),
            jnp.pad(masks.astype(bf16).reshape(1, 128), ((0, 15), (0, 0))),
        ]
    )
    recv = lax.all_gather(payload, "gy", axis_index_groups=alpha_groups())
    got = lax.dynamic_index_in_dim(recv[:, META + 32, :].reshape(BLOCKS, 16), alpha, 1, keepdims=False)

    dsq = jnp.sum(jnp.square(dets.astype(f32)), axis=2) * (-0.5 * SCALE) + 16.0 * LOG2E
    as_b = jnp.broadcast_to(dsq[:, :, None], (8, DBS, 128))

    vm = pl.BlockSpec(memory_space=pltpu.VMEM)
    sm = pl.BlockSpec(memory_space=pltpu.SMEM)
    hb = pl.BlockSpec(memory_space=pl.ANY)
    mom, mass, low, slots = pl.pallas_call(
        pair_kernel,
        out_shape=(
            jax.ShapeDtypeStruct((8, DBS, 128), f32),
            jax.ShapeDtypeStruct((8, DBS, 128), f32),
            jax.ShapeDtypeStruct((SLOTS, DBS, 256), bf16),
            jax.ShapeDtypeStruct((4, SLOTS), jnp.int32),
        ),
        in_specs=[sm, sm, vm, vm, vm],
        out_specs=(vm, vm, hb, sm),
        scratch_shapes=[
            pltpu.SMEM((8, BLOCKS + 8), jnp.int32),
            pltpu.VMEM((BLOCKS + 8, 128), f32),
            pltpu.VMEM((BLOCKS, 128), f32),
            pltpu.VMEM((2, DBS, 256), bf16),
            pltpu.SemaphoreType.DMA((2,)),
        ],
        compiler_params=pltpu.CompilerParams(vmem_limit_bytes=40 << 20),
        name="pairs",
    )(got.astype(jnp.int32), jnp.stack([gx, c]).astype(jnp.int32), recv, dets, as_b)

    part = jnp.sum(mass, axis=2) * DETECT_PROB
    part = part + jnp.pad(clutter.reshape(1, DBS), ((0, 7), (0, 0)))
    part = part.reshape(4, 2, DBS)
    other = core_swap(part)
    part = part + other[:, ::-1]
    norm = part
    for s in (1, 2, 3):
        norm = norm + jnp.roll(x_shift(part, s), s, axis=0)
    inv = (1.0 / norm).astype(bf16).astype(f32)
    inv_b = jnp.broadcast_to(inv.reshape(8, DBS)[:, :, None], (8, DBS, 128))

    share = pl.pallas_call(
        share_kernel,
        out_shape=jax.ShapeDtypeStruct((BLOCKS + 8, 128), f32),
        in_specs=[sm, vm, hb],
        out_specs=vm,
        scratch_shapes=[pltpu.VMEM((4, DBS, 256), bf16), pltpu.SemaphoreType.DMA((4,))],
        compiler_params=pltpu.CompilerParams(vmem_limit_bytes=24 << 20),
        name="shares",
    )(slots, inv_b, low)
    back = lax.all_to_all(
        share[:BLOCKS].reshape(16, 8, 128), "gy", split_axis=0, concat_axis=0, axis_index_groups=alpha_groups()
    )
    total = jnp.sum(back, axis=0).reshape(-1)
    updated = weights.astype(f32) * ((1.0 - DETECT_PROB) + DETECT_PROB * total)

    mom = mom.reshape(4, 2, DBS, 128)
    own = mom[:, 0] + core_swap(mom[:, 1])
    moment = own[0]
    for s in (1, 2, 3):
        moment = moment + x_shift(own[s], -s)
    normalizer = norm[0, 0]
    return updated, jnp.log(normalizer), DETECT_PROB * moment / normalizer[:, None]


def solution(mesh):
    both = P(("gx", "gy"))
    rows = P(("gx", "gy"), None)
    return jax.shard_map(
        local,
        mesh=mesh,
        in_specs=(rows, both, rows, both, rows, both),
        out_specs=(both, both, rows),
        check_vma=False,
    )
```

time: 311 us -> 181 us (0.58)
  matrix products: 105 us -> 0 us
  waiting for transfers between devices: 114 us -> 59.4 us
  Pallas kernels: 0 us -> 45.7 us
  other arithmetic: 35.1 us -> 8.92 us
  between operations: 0.85 us -> 14.3 us
  local copies, waits for them, and re-layouts: 20 us -> 10.7 us
  starting transfers between devices: 29.5 us -> 38.5 us
    all_to_all x3 -> x1, waiting for transfers between devices: 114 us -> 0.01 us  [local(): lax.all_to_all(share[:BLOCKS].reshape(16, 8, 128), 'gy', split_axis=0, co...]
    dot_general x48 -> x0, matrix products: 105 us -> none  [the longest x16 38.3 us: likelihood(): jnp.einsum('rf,df->rd', block_rows, detections, preferred_element_type=jn...]
    pallas_call x0 -> x2, Pallas kernels: none -> 45.7 us  [the longest x1 32.6 us: local(): pl.pallas_call(pair_kernel, out_shape=(jax.ShapeDtypeStruct((8, DBS, 128)...]
    all_gather x0 -> x1, waiting for transfers between devices: none -> 35.6 us  [local(): recv = lax.all_gather(payload, 'gy', axis_index_groups=alpha_groups())]
    ppermute x0 -> x12, waiting for transfers between devices: none -> 23.8 us  [the longest x9 22.3 us: x_shift(): return lax.ppermute(v, 'gx', [(i, (i + s) % 4) for i in range(4)])]
    ppermute x0 -> x12, starting transfers between devices: none -> 19.8 us  [the longest x9 19 us: x_shift(): return lax.ppermute(v, 'gx', [(i, (i + s) % 4) for i in range(4)])]
    reduce_sum x19 -> x5, other arithmetic: 22.6 us -> 4.1 us  [the longest x1 2.2 us: local(): part = jnp.sum(mass, axis=2) * DETECT_PROB]
    all_to_all x3 -> x1, starting transfers between devices: 29.5 us -> 18.7 us  [local(): lax.all_to_all(share[:BLOCKS].reshape(16, 8, 128), 'gy', split_axis=0, co...]
  transfers between devices with their start and end apart: 3 -> 14, of which waited for: 2 -> 9; matrix products, arithmetic and copies ran while one was open for 5% -> 5% of each run, Pallas kernels for 0% -> 7%
where the time goes in v1:
time: 181 us; the launch traced here: 178 us
  waiting for transfers between devices  59.4 us (33%)
  Pallas kernels  45.7 us (25%)
  starting transfers between devices  38.5 us (21%)
  between operations  14.3 us (8%)
  local copies, waits for them, and re-layouts  10.7 us (6%)
  other arithmetic  8.92 us (5%)
    all_gather x1, waiting for transfers between devices, local(): recv = lax.all_gather(payload, 'gy', axis_index_groups=alpha_groups())  35.6 us
    pallas_call x1, Pallas kernels, local(): pl.pallas_call(pair_kernel, out_shape=(jax.ShapeDtypeStruct((8, DBS, 128)...  32.6 us
    ppermute x9, waiting for transfers between devices, x_shift(): return lax.ppermute(v, 'gx', [(i, (i + s) % 4) for i in range(4)])  22.3 us
    ppermute x9, starting transfers between devices, x_shift(): return lax.ppermute(v, 'gx', [(i, (i + s) % 4) for i in range(4)])  19 us
    all_to_all x1, starting transfers between devices, local(): lax.all_to_all(share[:BLOCKS].reshape(16, 8, 128), 'gy', split_axis=0, co...  18.7 us
    pallas_call x1, Pallas kernels, local(): pl.pallas_call(share_kernel, out_shape=jax.ShapeDtypeStruct((BLOCKS + 8,...  13.1 us
    unnamed x16, local copies, waits for them, and re-layouts  6.98 us
  transfers between devices with their start and end apart: 14, of which 9 were waited for; matrix products, arithmetic and copies ran while one was open for 5% of the time, Pallas kernels for 7%

profile of v1, /device:TPU:0, one launch (start us, length us, event | category | flops | bytes accessed | tf_op | source)
XLA Modules:
  0.0 177.5 jit_solution(7799414695739124490)
XLA Ops:
  7.2 1.2 multiply_reduce_fusion.1
  8.4 1.0 constant_dynamic-update-slice_fusion.5
  11.9 0.9 constant_dynamic-update-slice_fusion.10
  13.4 0.9 pad_maximum_fusion
  14.4 1.6 collective-permute-start.1
  16.1 1.7 collective-permute-start.3
  17.8 1.9 %collective-permute-start.2 = (bf16[2,512,128]{2,1,0:T(8,128)(2,1)S(1)}, bf16[2,512,128]{2,1,0:T(8,128)(2,1)S(1)}, u32[]{:S(2)}, u32[]{:S(2)}) collective-permute-start(bf16[2,512,128]{2,1,0:T(8,128)(2,1)S(1)} %pad_maximum_fusion), channel_id=1, source_target_pairs={{0,64},{32,96},{64,0},{96,32},{1,65},{33,97},{65,1},{97,33},{2,66}... | collective-permute-start | bytes 786440 | tf_op jit(solution)/shard_map/ppermute | solution.py:31
  19.7 4.3 %collective-permute-done.1 = bf16[2,512,128]{2,1,0:T(8,128)(2,1)S(1)} collective-permute-done((bf16[2,512,128]{2,1,0:T(8,128)(2,1)S(1)}, bf16[2,512,128]{2,1,0:T(8,128)(2,1)S(1)}, u32[]{:S(2)}, u32[]{:S(2)}) %collective-permute-start.1) | collective-permute-done | bytes 262176 | tf_op jit(solution)/shard_map/ppermute | solution.py:31
  24.0 6.6 %collective-permute-done.2 = bf16[2,512,128]{2,1,0:T(8,128)(2,1)S(1)} collective-permute-done((bf16[2,512,128]{2,1,0:T(8,128)(2,1)S(1)}, bf16[2,512,128]{2,1,0:T(8,128)(2,1)S(1)}, u32[]{:S(2)}, u32[]{:S(2)}) %collective-permute-start.2) | collective-permute-done | bytes 262176 | tf_op jit(solution)/shard_map/ppermute | solution.py:31
  31.4 35.6 %all-gather.3.cloned.1.call-done = bf16[17152,128]{1,0:T(8,128)(2,1)} async-done(((bf16[1072,128]{1,0:T(8,128)(2,1)}), bf16[17152,128]{1,0:T(8,128)(2,1)}) %all-gather.3.cloned.1.call-update) | async-done | bytes 4390928 | tf_op jit(solution)/shard_map/all_gather | solution.py:170
  68.7 2.2 %copy-done = bf16[17152,128]{1,0:T(8,128)(2,1)S(1)} copy-done((bf16[17152,128]{1,0:T(8,128)(2,1)S(1)}, bf16[17152,128]{1,0:T(8,128)(2,1)}, u32[]{:S(2)}) %copy-start) | copy-done | bytes 4390936
  71.0 32.6 %pairs.1 = (f32[8,512,128]{2,1,0:T(8,128)S(1)}, f32[8,512,128]{2,1,0:T(8,128)S(1)}, bf16[136,512,256]{2,1,0:T(8,128)(2,1)}, s32[4,136]{1,0:T(4,128)S(1)}) custom-call(s32[128]{0:T(128)S(1)} %convert_reduce_fusion.mask_ref, s32[2]{0:T(128)S(1)} %pad_add_fusion.1.pos_ref, bf16[16,1072,128]{2,1,0:T(8,128)(2,1)S(1)} %bitcast.58, ...), custom_call_target="tpu_custom_call" | custom-call | tf_op jit(solution)/shard_map/pairs/pallas_call | solution.py:179
  103.6 1.4 copy-done.1
  105.1 2.2 %reduce_sum.48 = f32[8,512]{1,0:T(8,128)S(1)} reduce(f32[8,512,128]{2,1,0:T(8,128)} %copy-done.1, f32[]{:T(128)} %constant.78.clone.1), dimensions={2}, to_apply=%region_3.4 | reduce | flops 520192 | bytes 2113540 | tf_op jit(solution)/shard_map/reduce_sum | solution.py:200
  109.0 5.7 %collective-permute-start.7 = (f32[4,2,512]{2,1,0:T(2,128)S(1)}, f32[4,2,512]{2,1,0:T(2,128)S(1)}, u32[]{:S(2)}, u32[]{:S(2)}) collective-permute-start(f32[4,2,512]{2,1,0:T(2,128)S(1)} %add.82), channel_id=1, source_target_pairs={{0,96},{32,0},{64,32},{96,64},{1,97},{33,1},{65,33},{97,65},{2,98}... | collective-permute-start | bytes 49160 | tf_op jit(solution)/shard_map/ppermute | solution.py:31
  114.6 1.5 collective-permute-start.6
  116.2 3.4 %collective-permute-done.5 = f32[4,2,512]{2,1,0:T(2,128)S(1)} collective-permute-done((f32[4,2,512]{2,1,0:T(2,128)S(1)}, f32[4,2,512]{2,1,0:T(2,128)S(1)}, u32[]{:S(2)}, u32[]{:S(2)}) %collective-permute-start.5) | collective-permute-done | bytes 16416 | tf_op jit(solution)/shard_map/ppermute | solution.py:31
  120.5 13.1 %shares.1 = f32[136,128]{1,0:T(8,128)S(1)} custom-call(s32[4,136]{1,0:T(4,128)S(1)} %get-tuple-element.7.slot_ref, f32[8,512,128]{2,1,0:T(8,128)S(1)} %broadcast_in_dim.40.inv_ref, bf16[136,512,256]{2,1,0:T(8,128)(2,1)} %get-tuple-element.9.low_ref), custom_call_target="tpu_custom_call" | custom-call | tf_op jit(solution)/shard_map/shares/pallas_call | solution.py:211
  134.3 18.7 %all-to-all-start = ((f32[16,8,128]{2,1,0:T(8,128)}), f32[16,8,128]{2,1,0:T(8,128)S(1)}, u32[]{:S(2)}, u32[]{:S(2)}) async-start(f32[16,8,128]{2,1,0:T(8,128)} %slice_bitcast_fusion.6), calls=%async_computation | async-start | bytes 131072 | tf_op jit(solution)/shard_map/all_to_all | solution.py:220
  153.0 1.3 fusion
  154.4 5.1 %collective-permute-start.9 = (f32[512,128]{1,0:T(8,128)S(1)}, f32[512,128]{1,0:T(8,128)S(1)}, u32[]{:S(2)}, u32[]{:S(2)}) collective-permute-start(f32[512,128]{1,0:T(8,128)S(1)} %get-tuple-element.13), channel_id=1, source_target_pairs={{0,96},{32,0},{64,32},{96,64},{1,97},{33,1},{65,33},{97,65},{2,98}... | collective-permute-start | bytes 786440 | tf_op jit(solution)/shard_map/ppermute | solution.py:31
  159.5 1.5 collective-permute-start.10
  162.2 5.5 %collective-permute-done.9 = f32[512,128]{1,0:T(8,128)S(1)} collective-permute-done((f32[512,128]{1,0:T(8,128)S(1)}, f32[512,128]{1,0:T(8,128)S(1)}, u32[]{:S(2)}, u32[]{:S(2)}) %collective-permute-start.9) | collective-permute-done | bytes 262176 | tf_op jit(solution)/shard_map/ppermute | solution.py:31
  167.7 2.2 %collective-permute-done.11 = f32[512,128]{1,0:T(8,128)S(1)} collective-permute-done((f32[512,128]{1,0:T(8,128)S(1)}, f32[512,128]{1,0:T(8,128)S(1)}, u32[]{:S(2)}, u32[]{:S(2)}) %collective-permute-start.11) | collective-permute-done | bytes 262176 | tf_op jit(solution)/shard_map/ppermute | solution.py:31
  (63 shorter events, 11.1 us)
Async XLA Ops:
  7.2 59.9 %all-gather.3.cloned.1.call-start = ((), (), s32[]{:S(2)}) async-start(), calls=%async_computation.1 | async-start | bytes 4665344 | tf_op jit(solution)/shard_map/all_gather | solution.py:170
  11.1 0.7 copy-start.2
  11.8 1.6 collective-permute-start
  14.4 9.6 %collective-permute-start.1 = (bf16[2,512,128]{2,1,0:T(8,128)(2,1)S(1)}, bf16[2,512,128]{2,1,0:T(8,128)(2,1)S(1)}, u32[]{:S(2)}, u32[]{:S(2)}) collective-permute-start(bf16[2,512,128]{2,1,0:T(8,128)(2,1)S(1)} %pad_maximum_fusion), channel_id=1, source_target_pairs={{0,32},{32,64},{64,96},{96,0},{1,33},{33,65},{65,97},{97,1},{2,34}... | collective-permute-start | bytes 786440 | tf_op jit(solution)/shard_map/ppermute | solution.py:31
  16.1 14.6 %collective-permute-start.3 = (bf16[2,512,128]{2,1,0:T(8,128)(2,1)S(1)}, bf16[2,512,128]{2,1,0:T(8,128)(2,1)S(1)}, u32[]{:S(2)}, u32[]{:S(2)}) collective-permute-start(bf16[2,512,128]{2,1,0:T(8,128)(2,1)S(1)} %pad_maximum_fusion), channel_id=1, source_target_pairs={{0,96},{32,0},{64,32},{96,64},{1,97},{33,1},{65,33},{97,65},{2,98}... | collective-permute-start | bytes 786440 | tf_op jit(solution)/shard_map/ppermute | solution.py:31
  17.8 12.9 %collective-permute-start.2 = (bf16[2,512,128]{2,1,0:T(8,128)(2,1)S(1)}, bf16[2,512,128]{2,1,0:T(8,128)(2,1)S(1)}, u32[]{:S(2)}, u32[]{:S(2)}) collective-permute-start(bf16[2,512,128]{2,1,0:T(8,128)(2,1)S(1)} %pad_maximum_fusion), channel_id=1, source_target_pairs={{0,64},{32,96},{64,0},{96,32},{1,65},{33,97},{65,1},{97,33},{2,66}... | collective-permute-start | bytes 786440 | tf_op jit(solution)/shard_map/ppermute | solution.py:31
  68.7 2.3 %copy-start = (bf16[17152,128]{1,0:T(8,128)(2,1)S(1)}, bf16[17152,128]{1,0:T(8,128)(2,1)}, u32[]{:S(2)}) copy-start(bf16[17152,128]{1,0:T(8,128)(2,1)} %all-gather.3.cloned.1.call-done) | copy-start | bytes 13172740
  103.6 1.4 copy-start.1
  105.0 2.4 %copy-start.4 = (f32[512]{0:T(512)S(1)}, f32[512]{0:T(512)}, u32[]{:S(2)}) copy-start(f32[512]{0:T(512)} %param.9) | copy-start | bytes 6148
  105.0 47.9 %collective-permute-start.8 = (f32[4,512,128]{2,1,0:T(8,128)S(1)}, f32[4,512,128]{2,1,0:T(8,128)}, u32[]{:S(2)}, u32[]{:S(2)}) collective-permute-start(f32[4,512,128]{2,1,0:T(8,128)S(1)} %slice_bitcast_fusion), channel_id=1, source_target_pairs={{0,1},{1,0},{2,3},{3,2},{4,5},{5,4},{6,7},{7,6},{8,9},{9,8},{10,11... | collective-permute-start | bytes 3145736 | tf_op jit(solution)/shard_map/ppermute | solution.py:27
  107.4 1.4 collective-permute-start.4
  109.0 7.2 %collective-permute-start.7 = (f32[4,2,512]{2,1,0:T(2,128)S(1)}, f32[4,2,512]{2,1,0:T(2,128)S(1)}, u32[]{:S(2)}, u32[]{:S(2)}) collective-permute-start(f32[4,2,512]{2,1,0:T(2,128)S(1)} %add.82), channel_id=1, source_target_pairs={{0,96},{32,0},{64,32},{96,64},{1,97},{33,1},{65,33},{97,65},{2,98}... | collective-permute-start | bytes 49160 | tf_op jit(solution)/shard_map/ppermute | solution.py:31
  114.6 4.9 %collective-permute-start.5 = (f32[4,2,512]{2,1,0:T(2,128)S(1)}, f32[4,2,512]{2,1,0:T(2,128)S(1)}, u32[]{:S(2)}, u32[]{:S(2)}) collective-permute-start(f32[4,2,512]{2,1,0:T(2,128)S(1)} %add.82), channel_id=1, source_target_pairs={{0,32},{32,64},{64,96},{96,0},{1,33},{33,65},{65,97},{97,1},{2,34}... | collective-permute-start | bytes 49160 | tf_op jit(solution)/shard_map/ppermute | solution.py:31
  114.6 5.2 %collective-permute-start.6 = (f32[4,2,512]{2,1,0:T(2,128)S(1)}, f32[4,2,512]{2,1,0:T(2,128)S(1)}, u32[]{:S(2)}, u32[]{:S(2)}) collective-permute-start(f32[4,2,512]{2,1,0:T(2,128)S(1)} %add.82), channel_id=1, source_target_pairs={{0,64},{32,96},{64,0},{96,32},{1,65},{33,97},{65,1},{97,33},{2,66}... | collective-permute-start | bytes 49160 | tf_op jit(solution)/shard_map/ppermute | solution.py:31
  134.3 27.3 %all-to-all-start = ((f32[16,8,128]{2,1,0:T(8,128)}), f32[16,8,128]{2,1,0:T(8,128)S(1)}, u32[]{:S(2)}, u32[]{:S(2)}) async-start(f32[16,8,128]{2,1,0:T(8,128)} %slice_bitcast_fusion.6), calls=%async_computation | async-start | bytes 131072 | tf_op jit(solution)/shard_map/all_to_all | solution.py:220
  152.9 8.7 %copy-start.3 = (bf16[1024]{0:T(1024)(128)(2,1)S(1)}, bf16[1024]{0:T(1024)(128)(2,1)}, u32[]{:S(2)}) copy-start(bf16[1024]{0:T(1024)(128)(2,1)} %param.7) | copy-start | bytes 6148
  154.4 13.3 %collective-permute-start.9 = (f32[512,128]{1,0:T(8,128)S(1)}, f32[512,128]{1,0:T(8,128)S(1)}, u32[]{:S(2)}, u32[]{:S(2)}) collective-permute-start(f32[512,128]{1,0:T(8,128)S(1)} %get-tuple-element.13), channel_id=1, source_target_pairs={{0,96},{32,0},{64,32},{96,64},{1,97},{33,1},{65,33},{97,65},{2,98}... | collective-permute-start | bytes 786440 | tf_op jit(solution)/shard_map/ppermute | solution.py:31
  159.4 10.4 %collective-permute-start.11 = (f32[512,128]{1,0:T(8,128)S(1)}, f32[512,128]{1,0:T(8,128)S(1)}, u32[]{:S(2)}, u32[]{:S(2)}) collective-permute-start(f32[512,128]{1,0:T(8,128)S(1)} %get-tuple-element.14), channel_id=1, source_target_pairs={{0,32},{32,64},{64,96},{96,0},{1,33},{33,65},{65,97},{97,1},{2,34}... | collective-permute-start | bytes 786440 | tf_op jit(solution)/shard_map/ppermute | solution.py:31
  159.5 10.4 %collective-permute-start.10 = (f32[512,128]{1,0:T(8,128)S(1)}, f32[512,128]{1,0:T(8,128)S(1)}, u32[]{:S(2)}, u32[]{:S(2)}) collective-permute-start(f32[512,128]{1,0:T(8,128)S(1)} %get-tuple-element.15), channel_id=1, source_target_pairs={{0,64},{32,96},{64,0},{96,32},{1,65},{33,97},{65,1},{97,33},{2,66}... | collective-permute-start | bytes 786440 | tf_op jit(solution)/shard_map/ppermute | solution.py:31
Sparse Core Ops, SparseCore 0:
  11.9 55.0 all-gather.2

commit v2 on v1

v2 whole, which is shorter than its diff:
```python
import functools

import jax
import jax.numpy as jnp
from jax import lax
from jax.experimental import pallas as pl
from jax.experimental.pallas import tpu as pltpu
from jax.sharding import PartitionSpec as P

PBS = 128
DBS = 512
DETECT_PROB = 0.9
LOG2E = 1.4426950408889634
SCALE = LOG2E / 8.0
HB = 4
META = HB * PBS
ROWS = META + 32
TABLE = 152
LOW = 76
RING = 8
DUMMY = 8
NONE = 128

f32 = jnp.float32
bf16 = jnp.bfloat16


def alpha_groups():
    return [[a * 2 + c for a in range(16)] for c in range(2)]


def gy_shift(v, dz, dy, dc=0):
    perm = []
    for i in range(32):
        z, y, c = i // 8, i // 2 % 4, i % 2
        perm.append((i, (z + dz) % 4 * 8 + (y + dy) % 4 * 2 + (c + dc) % 2))
    return lax.ppermute(v, "gy", perm)


def x_shift(v, s):
    return lax.ppermute(v, "gx", [(i, (i + s) % 4) for i in range(4)])


def x_swap(v, s):
    return lax.ppermute(v, "gx", [(i, i ^ s) for i in range(4)])


def pair_kernel(steps, before, *refs):
    parts = 2 * len(steps)
    count = parts * 16
    pos_ref, refs = refs[0], refs[1:]
    part_refs, refs = refs[:parts], refs[parts:]
    det_ref, refs = refs[0], refs[1:]
    first = before == 0
    tables, refs = refs[:before], refs[before:]
    if not first:
        as_ref, refs = refs[0], refs[2:]
    mom_ref, mass_ref, low_ref, slot_ref, refs = refs[0], refs[1], refs[2], refs[3], refs[4:]
    if first:
        as_ref, refs = refs[0], refs[1:]
    lst, gates, grow, meta, xs, wrow, brow, cr0, cr1, w0, w1, ring, sem, xsem, msem = refs
    c, z, y = pos_ref[0], pos_ref[1], pos_ref[2]
    lane = (z * 4 + y) * HB

    heads = [
        pltpu.make_async_copy(part_refs[t].at[:, pl.ds(META, 32), :], meta.at[pl.ds(4 * t, 4)], msem.at[t])
        for t in range(parts)
    ]
    loads = [
        pltpu.make_async_copy(part_refs[t].at[:, pl.ds(0, META), :], xs.at[pl.ds(4 * t, 4)], xsem.at[t])
        for t in range(parts)
    ]
    for copy in heads + loads:
        copy.start()
    mom_ref[...] = jnp.zeros_like(mom_ref)
    mass_ref[...] = jnp.zeros_like(mass_ref)
    if first:
        for r in range(8):
            for h in range(0, DBS, 128):
                d = det_ref[r, h:h + 128, :].astype(f32)
                v = jnp.sum(d * d, axis=1, keepdims=True) * (-0.5 * SCALE) + 16.0 * LOG2E
                as_ref[r, h:h + 128, :] = jnp.broadcast_to(v, (128, 128))
    base = jnp.int32(0)
    for table in tables:
        base = base + (table[3, 0] + 1) // 2
    for copy in heads:
        copy.wait()
    for s in range(parts * 4):
        grow[s:s + 1, :] = meta[s, 16:32, :].astype(f32)[0:1].astype(jnp.int32)
    gate_load = pltpu.make_async_copy(grow, gates, msem.at[0])
    gate_load.start()
    for s in range(parts * 4):
        rows = meta[s, 0:16, :].astype(f32)
        wrow[s * 4:(s + 1) * 4, :] = rows[0:4]
        brow[s * 4:(s + 1) * 4, :] = rows[4:8] + rows[8:12] + rows[12:16]
    wrow[count:count + 8, :] = jnp.zeros((8, 128), f32)
    gate_load.wait()

    bits = [r ^ c for r in range(8)]
    counts = [jnp.int32(0)] * 8
    for s in range(parts * 4):
        h, step, u = s // 4 % 2, steps[s // 8], s % 4
        dz, dy = (step, u) if h == 0 else (u, step)
        home = (((z + 4 - dz) % 4) * 4 + (y + 4 - dy) % 4) * 8 + h * 4
        for j in range(HB):
            m = gates[s, lane + j]
            v = (home + j) * 256 + (s * 4 + j)
            for r in range(8):
                lst[r, counts[r]] = v
                counts[r] = counts[r] + ((m >> bits[r]) & 1)

    def put(q, v0, v1, r):
        slot_ref[0, q] = v0
        slot_ref[1, q] = v1
        slot_ref[2, q] = r

    hole = NONE * 256 + count
    put(0, 0, hole, DUMMY)
    q = jnp.int32(1)
    for r in range(8):
        cnt = counts[r]

        def fill(p, q, r=r, cnt=cnt):
            put(q, lst[r, 2 * p], jnp.where(2 * p + 1 < cnt, lst[r, 2 * p + 1], hole), r)
            return q + 1

        q = lax.fori_loop(0, (cnt + 1) // 2, fill, q)
    for d in range(3):
        put(q + d, NONE * 256, hole, DUMMY)
    n = q - 1
    slot_ref[3, 0] = n
    for copy in loads:
        copy.wait()

    cr, w = (cr0, cr1), (w0, w1)

    def copy_out(p, j):
        return pltpu.make_async_copy(ring.at[j], low_ref.at[p], sem.at[j])

    def both(q):
        b0 = slot_ref[0, q] & 255
        b1 = jnp.minimum(slot_ref[1, q] & 255, count - 1)
        return jnp.concatenate(
            [xs[b // 4, pl.ds(pl.multiple_of(b % 4 * PBS, PBS), PBS), :] for b in (b0, b1)], axis=0
        )

    def cross(q, s):
        r = jnp.minimum(slot_ref[2, q], 7)
        cr[s][...] = lax.dot_general(det_ref[r], both(q), (((1,), (1,)), ((), ())), preferred_element_type=f32)

    def likelihood(q, s, j):
        b0, b1, r = slot_ref[0, q] & 255, slot_ref[1, q] & 255, slot_ref[2, q]
        b1c, rc = jnp.minimum(b1, count - 1), jnp.minimum(r, 7)
        w2 = jnp.concatenate([wrow[pl.ds(b0, 1), :], wrow[pl.ds(b1, 1), :]], axis=1)
        s2 = jnp.concatenate([brow[pl.ds(b0, 1), :], brow[pl.ds(b1c, 1), :]], axis=1)
        for h in range(0, DBS, 32):
            rows = slice(h, h + 32)
            a = as_ref[rc, rows, :]
            lik = jnp.exp2(cr[s][rows, :] * SCALE + (jnp.concatenate([a, a], axis=1) + s2))
            ring[j, 1 - s, rows, :] = lik.astype(bf16)
            wtd = lik * w2
            mass_ref[r, rows, :] += wtd[:, :128] + wtd[:, 128:]
            w[s][rows, :] = wtd.astype(bf16)

    def moment(q, s):
        r = slot_ref[2, q]
        mom_ref[jnp.where(r < DUMMY, r // 2 + r % 2 * 4, DUMMY)] += jnp.dot(w[s][...], both(q), preferred_element_type=f32)

    cross(1, 1)

    def body(p, carry):
        q = 2 * p + 2
        j = lax.rem(p, RING)

        @pl.when(p >= RING)
        def _():
            copy_out(0, j).wait()

        cross(q, 0)
        likelihood(q - 1, 1, j)
        moment(q - 2, 0)
        cross(q + 1, 1)
        likelihood(q, 0, j)
        moment(q - 1, 1)
        copy_out(base + p, j).start()
        return carry

    total = (n + 2) // 2
    lax.fori_loop(0, total, body, 0)

    def drain(j, carry):
        copy_out(0, j).wait()
        return carry

    lax.fori_loop(0, jnp.minimum(total, RING), drain, 0)


def pair_call(steps, pos, parts, dets, tables, state):
    n = len(parts)
    first = state is None
    vm = pl.BlockSpec(memory_space=pltpu.VMEM)
    sm = pl.BlockSpec(memory_space=pltpu.SMEM)
    hb = pl.BlockSpec(memory_space=pl.ANY)
    acc = jax.ShapeDtypeStruct((9, DBS, 128), f32)
    low = jax.ShapeDtypeStruct((LOW, 2, DBS, 256), bf16)
    table = jax.ShapeDtypeStruct((4, TABLE), jnp.int32)
    operands, specs = [pos] + parts + [dets], [sm] + [hb] * n + [vm]
    outs, out_specs = [acc, acc, low, table], [vm, vm, hb, sm]
    aliases = {}
    if first:
        outs, out_specs = outs + [jax.ShapeDtypeStruct((8, DBS, 128), f32)], out_specs + [vm]
    else:
        operands += tables + list(state)
        specs += [sm] * len(tables) + [vm, hb]
        aliases = {len(specs) - 1: 2}
    work = 26 * n // 2
    return pl.pallas_call(
        functools.partial(pair_kernel, steps, len(tables)),
        out_shape=outs,
        in_specs=specs,
        out_specs=out_specs,
        scratch_shapes=[
            pltpu.SMEM((8, n * 16 + 8), jnp.int32),
            pltpu.SMEM((n * 4, 128), jnp.int32),
            pltpu.VMEM((n * 4, 128), jnp.int32),
            pltpu.VMEM((n * 4, 32, 128), bf16),
            pltpu.VMEM((n * 4, META, 128), bf16),
            pltpu.VMEM((n * 16 + 8, 128), f32),
            pltpu.VMEM((n * 16, 128), f32),
            pltpu.VMEM((DBS, 256), f32),
            pltpu.VMEM((DBS, 256), f32),
            pltpu.VMEM((DBS, 256), bf16),
            pltpu.VMEM((DBS, 256), bf16),
            pltpu.VMEM((RING, 2, DBS, 256), bf16),
            pltpu.SemaphoreType.DMA((RING,)),
            pltpu.SemaphoreType.DMA((n,)),
            pltpu.SemaphoreType.DMA((n,)),
        ],
        input_output_aliases=aliases,
        compiler_params=pltpu.CompilerParams(vmem_limit_bytes=14 << 20),
        cost_estimate=pl.CostEstimate(
            flops=work * 4 * DBS * PBS * 128, transcendentals=work * DBS * PBS, bytes_accessed=work * DBS * PBS * 2
        ),
        name="pairs",
    )(*operands)


def share_kernel(ta, tb, tc, inv_ref, low_ref, out_ref, share_ref, buf, sem):
    share_ref[...] = jnp.zeros_like(share_ref)
    depth = buf.shape[0]
    na, nb, nc = [(t[3, 0] + 1) // 2 for t in (ta, tb, tc)]
    n = na + nb + nc

    def entry(k, p, e):
        ea = jnp.minimum(2 * p + e, TABLE - 1)
        eb = jnp.clip(2 * (p - na) + e, 0, TABLE - 1)
        ec = jnp.maximum(2 * (p - na - nb) + e, 0)
        return jnp.where(p < na, ta[k, ea], jnp.where(p < na + nb, tb[k, eb], tc[k, ec]))

    def copy_in(p, s):
        return pltpu.make_async_copy(low_ref.at[p], buf.at[s], sem.at[s])

    for d in range(depth):
        @pl.when(d < n)
        def _(d=d):
            copy_in(d, d).start()

    def one(p, s, e):
        a0, a1 = entry(0, p, e + 1) >> 8, entry(1, p, e + 1) >> 8
        r = jnp.minimum(entry(2, p, e + 1), 7)
        acc = jnp.zeros((8, 256), f32)
        for h in range(0, DBS, 64):
            v = inv_ref[r, h:h + 64, :]
            t = buf[s, e, h:h + 64, :].astype(f32) * jnp.concatenate([v, v], axis=1)
            acc = acc + jnp.sum(t.reshape(8, 8, 256), axis=0)
        return a0, a1, jnp.sum(acc, axis=0, keepdims=True)

    def step(p, carry):
        s = lax.rem(p, depth)
        copy_in(p, s).wait()
        done = [one(p, s, 0), one(p, s, 1)]
        for a0, a1, t in done:
            share_ref[pl.ds(a0, 1), :] += t[:, :128]
            share_ref[pl.ds(a1, 1), :] += t[:, 128:]

        @pl.when(p + depth < n)
        def _():
            copy_in(p + depth, s).start()

        return carry

    lax.fori_loop(0, n, step, 0)
    out_ref[...] = share_ref[0:NONE, :]


def share_call(tables, inv_b, low):
    vm = pl.BlockSpec(memory_space=pltpu.VMEM)
    sm = pl.BlockSpec(memory_space=pltpu.SMEM)
    hb = pl.BlockSpec(memory_space=pltpu.HBM)
    return pl.pallas_call(
        share_kernel,
        out_shape=jax.ShapeDtypeStruct((NONE, 128), f32),
        in_specs=[sm, sm, sm, vm, hb],
        out_specs=vm,
        scratch_shapes=[
            pltpu.VMEM((NONE + 8, 128), f32),
            pltpu.VMEM((RING, 2, DBS, 256), bf16),
            pltpu.SemaphoreType.DMA((RING,)),
        ],
        compiler_params=pltpu.CompilerParams(vmem_limit_bytes=30 << 20),
        cost_estimate=pl.CostEstimate(flops=104 * DBS * PBS * 2, transcendentals=0, bytes_accessed=104 * DBS * PBS * 2),
        name="shares",
    )(*tables, inv_b, low)


def local(particles, weights, detections, clutter, gate_ids, gate_lens):
    gx, gy = lax.axis_index("gx"), lax.axis_index("gy")
    c, alpha = gy % 2, gy // 2
    pos = jnp.stack([c, gy // 8, gy // 2 % 4]).astype(jnp.int32)

    half = jnp.sum(jnp.square(particles.astype(f32)), axis=1).reshape(8, PBS) * (-0.5 * SCALE)
    hi = lax.reduce_precision(half, 8, 7)
    mid = lax.reduce_precision(half - hi, 8, 7)
    lo = (half - hi) - mid
    live = jnp.arange(16, dtype=jnp.int32)[None, :] < gate_lens[:, None]
    bit = jnp.where(live, 1 << ((gate_ids // 32) * 2 + gate_ids % 2), 0)
    owner = (gate_ids % 32) // 2
    masks = jnp.sum(jnp.where(owner[:, None, :] == jnp.arange(16)[None, :, None], bit[:, None, :], 0), axis=2)
    rows = [weights.reshape(8, PBS), hi.astype(bf16), mid.astype(bf16), lo.astype(bf16)]
    sends = []
    for h in range(2):
        own = slice(h * HB, (h + 1) * HB)
        gate = jnp.transpose(masks[own]).reshape(1, 64).astype(bf16)
        sends.append(
            jnp.concatenate(
                [particles[h * META:(h + 1) * META]]
                + [v[own] for v in rows]
                + [jnp.pad(gate, ((0, 15), (0, 64)))]
            )
        )

    dets = lax.all_gather(jnp.stack([detections, gy_shift(detections, 0, 0, 1)]), "gx").reshape(8, DBS, 128)

    sends = lax.optimization_barrier(sends)
    first = [
        [sends[0]] + [gy_shift(sends[0], 0, s) for s in (1, 3, 2)],
        [sends[1]] + [gy_shift(sends[1], s, 0) for s in (1, 3, 2)],
    ]
    first = lax.optimization_barrier(first)
    halves = [jnp.stack([v[0], v[1], v[3], v[2]]) for v in first]

    second = [v for s in (1, 3) for v in (gy_shift(halves[0], s, 0), gy_shift(halves[1], 0, s))]
    mom1, mass1, low, ta, as_b = pair_call((0,), pos, halves, dets, [], None)
    sum1 = jnp.sum(mass1, axis=2)
    second, halves, sum1 = lax.optimization_barrier((second, halves, sum1))
    third = [gy_shift(halves[0], 2, 0), gy_shift(halves[1], 0, 2)]
    mom2, mass2, low, tb = pair_call((1, 3), pos, second, dets, [ta], (as_b, low))
    mom3, mass3, low, tc = pair_call((2,), pos, third, dets, [ta, tb], (as_b, low))

    part = (sum1 + jnp.sum(mass2 + mass3, axis=2))[:8].reshape(4, 2, DBS) * DETECT_PROB
    mine = (jnp.arange(4)[:, None, None] == gx) & (jnp.arange(2)[None, :, None] == 0)
    part = part + jnp.where(mine, clutter[None, None, :], 0.0)
    norm = part + gy_shift(part, 0, 0, 1)[:, ::-1]
    norm = norm + x_swap(norm, 1)
    norm = norm + x_swap(norm, 2)
    inv = (1.0 / norm).astype(bf16).astype(f32)
    inv_b = jnp.broadcast_to(inv.reshape(8, DBS)[:, :, None], (8, DBS, 128))

    far = mom1[4:8] + mom2[4:8] + mom3[4:8]
    own = mom1[0:4] + mom2[0:4] + mom3[0:4] + gy_shift(far, 0, 0, 1)
    inv_b, own = lax.optimization_barrier((inv_b, own))
    moment = lax.dynamic_index_in_dim(own, gx, 0, False)
    for s in (1, 2, 3):
        moment = moment + x_shift(lax.dynamic_index_in_dim(own, (gx + s) % 4, 0, False), s)
    normalizer = lax.dynamic_index_in_dim(norm[:, 0], gx, 0, False)

    share = share_call((ta, tb, tc), inv_b, low)
    share, moment = lax.optimization_barrier((share, moment))
    back = lax.all_to_all(
        share.reshape(16, 8, 128), "gy", split_axis=0, concat_axis=0, axis_index_groups=alpha_groups()
    )
    total = jnp.sum(back, axis=0).reshape(-1)
    updated = weights.astype(f32) * ((1.0 - DETECT_PROB) + DETECT_PROB * total)
    return updated, jnp.log(normalizer), DETECT_PROB * moment / normalizer[:, None]


def solution(mesh):
    both = P(("gx", "gy"))
    rows = P(("gx", "gy"), None)
    return jax.shard_map(
        local,
        mesh=mesh,
        in_specs=(rows, both, rows, both, rows, both),
        out_specs=(both, both, rows),
        check_vma=False,
    )
```

time: 181 us -> 137 us (0.76); the launches traced: 178 us -> 137 us
  waiting for transfers between devices: 59.4 us -> 19.6 us
  other arithmetic: 8.92 us -> 15.8 us
  Pallas kernels: 45.7 us -> 39.6 us
  local copies, waits for them, and re-layouts: 10.7 us -> 8.7 us
    all_gather x1, waiting for transfers between devices: 35.6 us -> 0.16 us  [local(): lax.all_gather(jnp.stack([detections, gy_shift(detections, 0, 0, 1)]), 'gx')]
    ppermute x3 -> x17, starting transfers between devices: 0.75 us -> 28.4 us  [the longest x15 22 us: gy_shift(): return lax.ppermute(v, 'gy', perm)]
    ppermute x9 -> x3, waiting for transfers between devices: 22.3 us -> 1.03 us  [x_shift(): return lax.ppermute(v, 'gx', [(i, (i + s) % 4) for i in range(4)])]
    ppermute x9 -> x3, starting transfers between devices: 19 us -> 5.05 us  [x_shift(): return lax.ppermute(v, 'gx', [(i, (i + s) % 4) for i in range(4)])]
    all_to_all x1, starting transfers between devices: 18.7 us -> 5.71 us  [local(): lax.all_to_all(share.reshape(16, 8, 128), 'gy', split_axis=0, concat_axis...]
    ppermute x3 -> x17, waiting for transfers between devices: 1.45 us -> 11.6 us  [the longest x15 7.02 us: gy_shift(): return lax.ppermute(v, 'gy', perm)]
    all_to_all x1, waiting for transfers between devices: 0.01 us -> 6.82 us  [local(): lax.all_to_all(share.reshape(16, 8, 128), 'gy', split_axis=0, concat_axis...]
    pallas_call x2 -> x4, Pallas kernels: 45.7 us -> 39.6 us  [the longest x3 32.2 us: pair_call(): pl.pallas_call(functools.partial(pair_kernel, steps, len(tables)), out_sh...]
  transfers between devices with their start and end apart: 14 -> 22, of which waited for: 9 -> 11; matrix products, arithmetic and copies ran while one was open for 5% -> 8% of each run, Pallas kernels for 7% -> 23%
where the time goes in v2:
time: 137 us
  Pallas kernels  39.6 us (29%)
  starting transfers between devices  39.2 us (29%)
  waiting for transfers between devices  19.6 us (14%)
  other arithmetic  15.8 us (12%)
  between operations  14.4 us (11%)
  local copies, waits for them, and re-layouts  8.7 us (6%)
    pallas_call x3, Pallas kernels, pair_call(): pl.pallas_call(functools.partial(pair_kernel, steps, len(tables)), out_sh...  32.2 us
    ppermute x15, starting transfers between devices, gy_shift(): return lax.ppermute(v, 'gy', perm)  22 us
    pallas_call x1, Pallas kernels, share_call(): pl.pallas_call(share_kernel, out_shape=jax.ShapeDtypeStruct((NONE, 128),...  7.4 us
    ppermute x15, waiting for transfers between devices, gy_shift(): return lax.ppermute(v, 'gy', perm)  7.02 us
    all_to_all x1, waiting for transfers between devices, local(): lax.all_to_all(share.reshape(16, 8, 128), 'gy', split_axis=0, concat_axis...  6.82 us
    ppermute x2, starting transfers between devices, x_swap(): return lax.ppermute(v, 'gx', [(i, i ^ s) for i in range(4)])  6.48 us
    all_to_all x1, starting transfers between devices, local(): lax.all_to_all(share.reshape(16, 8, 128), 'gy', split_axis=0, concat_axis...  5.71 us
    ppermute x3, starting transfers between devices, x_shift(): return lax.ppermute(v, 'gx', [(i, (i + s) % 4) for i in range(4)])  5.05 us
  transfers between devices with their start and end apart: 22, of which 11 were waited for; matrix products, arithmetic and copies ran while one was open for 8% of the time, Pallas kernels for 23%

profile of v2, /device:TPU:0, one launch (start us, length us, event | category | flops | bytes accessed | tf_op | source)
XLA Modules:
  0.0 137.3 jit_solution(17051055273613607004)
XLA Ops:
  16.8 2.1 %collective-permute-start.2 = (bf16[544,128]{1,0:T(8,128)(2,1)S(1)}, bf16[544,128]{1,0:T(8,128)(2,1)S(1)}, u32[]{:S(2)}, u32[]{:S(2)}) collective-permute-start(bf16[544,128]{1,0:T(8,128)(2,1)S(1)} %concatenate.6), channel_id=1, source_target_pairs={{0,4},{1,5},{2,6},{3,7},{4,0},{5,1},{6,2},{7,3},{8,12},{9,13},{10,... | collective-permute-start | bytes 417800 | tf_op jit(solution)/shard_map/ppermute | solution.py:37
  18.9 1.9 %collective-permute-start.3 = (bf16[544,128]{1,0:T(8,128)(2,1)S(1)}, bf16[544,128]{1,0:T(8,128)(2,1)S(1)}, u32[]{:S(2)}, u32[]{:S(2)}) collective-permute-start(bf16[544,128]{1,0:T(8,128)(2,1)S(1)} %concatenate.7), channel_id=1, source_target_pairs={{0,8},{1,9},{2,10},{3,11},{4,12},{5,13},{6,14},{7,15},{8,16},{9,17... | collective-permute-start | bytes 417800 | tf_op jit(solution)/shard_map/ppermute | solution.py:37
  20.8 2.1 %collective-permute-start.4 = (bf16[544,128]{1,0:T(8,128)(2,1)S(1)}, bf16[544,128]{1,0:T(8,128)(2,1)S(1)}, u32[]{:S(2)}, u32[]{:S(2)}) collective-permute-start(bf16[544,128]{1,0:T(8,128)(2,1)S(1)} %concatenate.7), channel_id=1, source_target_pairs={{0,24},{1,25},{2,26},{3,27},{4,28},{5,29},{6,30},{7,31},{8,0},{9,1... | collective-permute-start | bytes 417800 | tf_op jit(solution)/shard_map/ppermute | solution.py:37
  23.0 2.0 %collective-permute-start.5 = (bf16[544,128]{1,0:T(8,128)(2,1)S(1)}, bf16[544,128]{1,0:T(8,128)(2,1)S(1)}, u32[]{:S(2)}, u32[]{:S(2)}) collective-permute-start(bf16[544,128]{1,0:T(8,128)(2,1)S(1)} %concatenate.7), channel_id=1, source_target_pairs={{0,16},{1,17},{2,18},{3,19},{4,20},{5,21},{6,22},{7,23},{8,24},{9,... | collective-permute-start | bytes 417800 | tf_op jit(solution)/shard_map/ppermute | solution.py:37
  26.4 2.3 %collective-permute-done.4 = bf16[544,128]{1,0:T(8,128)(2,1)S(1)} collective-permute-done((bf16[544,128]{1,0:T(8,128)(2,1)S(1)}, bf16[544,128]{1,0:T(8,128)(2,1)S(1)}, u32[]{:S(2)}, u32[]{:S(2)}) %collective-permute-start.4) | collective-permute-done | bytes 139296 | tf_op jit(solution)/shard_map/ppermute | solution.py:37
  28.7 1.9 %collective-permute-done.5 = bf16[544,128]{1,0:T(8,128)(2,1)S(1)} collective-permute-done((bf16[544,128]{1,0:T(8,128)(2,1)S(1)}, bf16[544,128]{1,0:T(8,128)(2,1)S(1)}, u32[]{:S(2)}, u32[]{:S(2)}) %collective-permute-start.5) | collective-permute-done | bytes 139296 | tf_op jit(solution)/shard_map/ppermute | solution.py:37
  35.5 2.1 %collective-permute-start.9 = (bf16[4,544,128]{2,1,0:T(8,128)(2,1)}, bf16[4,544,128]{2,1,0:T(8,128)(2,1)}, u32[]{:S(2)}, u32[]{:S(2)}) collective-permute-start(bf16[4,544,128]{2,1,0:T(8,128)(2,1)} %pad_maximum_fusion.refs_1_), channel_id=1, source_target_pairs={{0,24},{1,25},{2,26},{3,27},{4,28},{5,29},{6,30},{7,31},{8,0},{9,1... | collective-permute-start | bytes 1671176 | tf_op jit(solution)/shard_map/ppermute | solution.py:37
  39.1 9.8 %pairs.3 = (f32[9,512,128]{2,1,0:T(8,128)S(1)}, f32[9,512,128]{2,1,0:T(8,128)S(1)}, bf16[76,2,512,256]{3,2,1,0:T(8,128)(2,1)}, s32[4,152]{1,0:T(4,128)S(1)}, f32[8,512,128]{2,1,0:T(8,128)S(1)}) custom-call(s32[3]{0:T(128)S(1)} %pad_add_fusion.refs_0_, bf16[4,544,128]{2,1,0:T(8,128)(2,1)} %pad_maximum_fusion.refs_1_, ...), custom_call_target="tpu_custom_call" | custom-call | flops 872415232 | bytes 3407872 | tf_op jit(solution)/shard_map/pairs/pallas_call | solution.py:217
  51.8 2.3 %reduce_sum.47 = f32[9,512]{1,0:T(8,128)S(1)} reduce(f32[9,512,128]{2,1,0:T(8,128)} %copy-done.2, f32[]{:T(128)} %constant.126.clone.1), dimensions={2}, to_apply=%region_2.3 | reduce | flops 585216 | bytes 2377732 | tf_op jit(solution)/shard_map/reduce_sum | solution.py:354
  54.2 2.7 %collective-permute-start.11 = (bf16[4,544,128]{2,1,0:T(8,128)(2,1)}, bf16[4,544,128]{2,1,0:T(8,128)(2,1)S(1)}, u32[]{:S(2)}, u32[]{:S(2)}) collective-permute-start(bf16[4,544,128]{2,1,0:T(8,128)(2,1)} %pad_maximum_fusion.refs_1_), channel_id=1, source_target_pairs={{0,16},{1,17},{2,18},{3,19},{4,20},{5,21},{6,22},{7,23},{8,24},{9,... | collective-permute-start | bytes 1671176 | tf_op jit(solution)/shard_map/ppermute | solution.py:37
  56.9 1.9 %collective-permute-start.12 = (bf16[4,544,128]{2,1,0:T(8,128)(2,1)}, bf16[4,544,128]{2,1,0:T(8,128)(2,1)S(1)}, u32[]{:S(2)}, u32[]{:S(2)}) collective-permute-start(bf16[4,544,128]{2,1,0:T(8,128)(2,1)} %pad_maximum_fusion.1.refs_2_), channel_id=1, source_target_pairs={{0,4},{1,5},{2,6},{3,7},{4,0},{5,1},{6,2},{7,3},{8,12},{9,13},{10,... | collective-permute-start | bytes 1671176 | tf_op jit(solution)/shard_map/ppermute | solution.py:37
  58.9 13.9 %pairs.4 = (f32[9,512,128]{2,1,0:T(8,128)S(1)}, f32[9,512,128]{2,1,0:T(8,128)S(1)}, bf16[76,2,512,256]{3,2,1,0:T(8,128)(2,1)}, s32[4,152]{1,0:T(4,128)S(1)}) custom-call(s32[3]{0:T(128)S(1)} %pad_add_fusion.refs_0_, bf16[4,544,128]{2,1,0:T(8,128)(2,1)} %collective-permute-done.7.refs_1_, ...), custom_call_target="tpu_custom_call", output_to_operand_aliasing={{2}: (8, {})} | custom-call | flops 1744830464 | bytes 6815744 | tf_op jit(solution)/shard_map/pairs/pallas_call | solution.py:217
  72.8 8.5 %pairs.5 = (f32[9,512,128]{2,1,0:T(8,128)S(1)}, f32[9,512,128]{2,1,0:T(8,128)S(1)}, bf16[76,2,512,256]{3,2,1,0:T(8,128)(2,1)}, s32[4,152]{1,0:T(4,128)S(1)}) custom-call(s32[3]{0:T(128)S(1)} %pad_add_fusion.refs_0_, bf16[4,544,128]{2,1,0:T(8,128)(2,1)S(1)} %collective-permute-done.11.refs_1_, ...), custom_call_target="tpu_custom_call", output_to_operand_aliasing={{2}: (7, {})} | custom-call | flops 872415232 | bytes 3407872 | tf_op jit(solution)/shard_map/pairs/pallas_call | solution.py:217
  81.4 2.2 %slice_add_fusion = f32[4,512,128]{2,1,0:T(8,128)S(1)} fusion(f32[9,512,128]{2,1,0:T(8,128)S(1)} %get-tuple-element.65, f32[9,512,128]{2,1,0:T(8,128)S(1)} %get-tuple-element.64, f32[9,512,128]{2,1,0:T(8,128)} %copy-done.3), kind=kLoop, calls=%fused_computation.1 | loop fusion | flops 524288 | bytes 4194304 | tf_op jit(solution)/shard_map/add | solution.py:369
  86.6 4.0 %collective-permute-start.14 = (f32[4,2,512]{2,1,0:T(2,128)S(1)}, f32[4,2,512]{2,1,0:T(2,128)S(1)}, u32[]{:S(2)}, u32[]{:S(2)}) collective-permute-start(f32[4,2,512]{2,1,0:T(2,128)S(1)} %fusion.18), channel_id=1, source_target_pairs={{0,32},{32,0},{64,96},{96,64},{1,33},{33,1},{65,97},{97,65},{2,34}... | collective-permute-start | bytes 49160 | tf_op jit(solution)/shard_map/ppermute | solution.py:45
  90.6 1.7 %collective-permute-done.14 = f32[4,2,512]{2,1,0:T(2,128)S(1)} collective-permute-done((f32[4,2,512]{2,1,0:T(2,128)S(1)}, f32[4,2,512]{2,1,0:T(2,128)S(1)}, u32[]{:S(2)}, u32[]{:S(2)}) %collective-permute-start.14) | collective-permute-done | bytes 16416 | tf_op jit(solution)/shard_map/ppermute | solution.py:45
  92.3 2.5 %collective-permute-start.15 = (f32[4,2,512]{2,1,0:T(2,128)S(1)}, f32[4,2,512]{2,1,0:T(2,128)S(1)}, u32[]{:S(2)}, u32[]{:S(2)}) collective-permute-start(f32[4,2,512]{2,1,0:T(2,128)S(1)} %add.121), channel_id=1, source_target_pairs={{0,64},{32,96},{64,0},{96,32},{1,65},{33,97},{65,1},{97,33},{2,66}... | collective-permute-start | bytes 49160 | tf_op jit(solution)/shard_map/ppermute | solution.py:45
  94.8 2.8 %collective-permute-done.15 = f32[4,2,512]{2,1,0:T(2,128)S(1)} collective-permute-done((f32[4,2,512]{2,1,0:T(2,128)S(1)}, f32[4,2,512]{2,1,0:T(2,128)S(1)}, u32[]{:S(2)}, u32[]{:S(2)}) %collective-permute-start.15) | collective-permute-done | bytes 16416 | tf_op jit(solution)/shard_map/ppermute | solution.py:45
  97.7 2.1 %add_add_fusion = f32[4,512,128]{2,1,0:T(8,128)S(1)} fusion(f32[4,512,128]{2,1,0:T(8,128)S(1)} %collective-permute-done.16, f32[9,512,128]{2,1,0:T(8,128)} %copy-done.5, f32[9,512,128]{2,1,0:T(8,128)} %copy-done.4, f32[9,512,128]{2,1,0:T(8,128)} %copy-done.3), kind=kLoop, calls=%fused_computation.2 | loop fusion | flops 786432 | bytes 5242880 | tf_op jit(solution)/shard_map/add | solution.py:370
  101.2 2.0 %collective-permute-start.17 = (f32[512,128]{1,0:T(8,128)}, f32[512,128]{1,0:T(8,128)}, u32[]{:S(2)}, u32[]{:S(2)}) collective-permute-start(f32[512,128]{1,0:T(8,128)} %get-tuple-element.73), channel_id=1, source_target_pairs={{0,32},{32,64},{64,96},{96,0},{1,33},{33,65},{65,97},{97,1},{2,34}... | collective-permute-start | bytes 786440 | tf_op jit(solution)/shard_map/ppermute | solution.py:41
  103.8 2.4 %collective-permute-start.19 = (f32[512,128]{1,0:T(8,128)S(1)}, f32[512,128]{1,0:T(8,128)}, u32[]{:S(2)}, u32[]{:S(2)}) collective-permute-start(f32[512,128]{1,0:T(8,128)S(1)} %get-tuple-element.74), channel_id=1, source_target_pairs={{0,96},{32,0},{64,32},{96,64},{1,97},{33,1},{65,33},{97,65},{2,98}... | collective-permute-start | bytes 786440 | tf_op jit(solution)/shard_map/ppermute | solution.py:41
  106.8 7.4 %shares.1 = f32[128,128]{1,0:T(8,128)} custom-call(s32[4,152]{1,0:T(4,128)S(1)} %get-tuple-element.47.refs_6_.refs_4_.ta, s32[4,152]{1,0:T(4,128)S(1)} %get-tuple-element.55.refs_5_.tb, s32[4,152]{1,0:T(4,128)S(1)} %get-tuple-element.59.tc, f32[8,512,128]{2,1,0:T(8,128)S(1)} %broadcast_in_dim.60.inv_ref, bf16[76,2,512,256]{3,2,1,0:T(8,128)(2,1)} %get-tuple-element.67.low_ref), custom_call_target="tpu_custom_call" | custom-call | flops 13631488 | bytes 13631488 | tf_op jit(solution)/shard_map/shares/pallas_call | solution.py:300
  116.4 5.7 %all-to-all-start = ((f32[16,8,128]{2,1,0:T(8,128)}), f32[16,8,128]{2,1,0:T(8,128)S(1)}, u32[]{:S(2)}, u32[]{:S(2)}) async-start(f32[16,8,128]{2,1,0:T(8,128)} %bitcast.22), calls=%async_computation | async-start | bytes 131072 | tf_op jit(solution)/shard_map/all_to_all | solution.py:379
  123.0 6.8 %all-to-all-done = f32[16,8,128]{2,1,0:T(8,128)S(1)} async-done(((f32[16,8,128]{2,1,0:T(8,128)}), f32[16,8,128]{2,1,0:T(8,128)S(1)}, u32[]{:S(2)}, u32[]{:S(2)}) %all-to-all-start) | async-done | bytes 65568 | tf_op jit(solution)/shard_map/all_to_all | solution.py:379
  (87 shorter events, 29.8 us)
Async XLA Ops:
  7.2 30.7 %all-gather.3.cloned.1.call-start = ((), (), s32[]{:S(2)}) async-start(), calls=%async_computation.1 | async-start | bytes 1310720 | tf_op jit(solution)/shard_map/all_gather | solution.py:342
  7.2 2.3 %collective-permute-start.6 = (bf16[512,128]{1,0:T(8,128)(2,1)}, bf16[512,128]{1,0:T(8,128)(2,1)S(1)}, u32[]{:S(2)}, u32[]{:S(2)}) collective-permute-start(bf16[512,128]{1,0:T(8,128)(2,1)} %param.8), channel_id=1, source_target_pairs={{0,1},{1,0},{2,3},{3,2},{4,5},{5,4},{6,7},{7,6},{8,9},{9,8},{10,11... | collective-permute-start | bytes 393224 | tf_op jit(solution)/shard_map/ppermute | solution.py:37
  13.6 9.4 %collective-permute-start = (bf16[544,128]{1,0:T(8,128)(2,1)S(1)}, bf16[544,128]{1,0:T(8,128)(2,1)S(1)}, u32[]{:S(2)}, u32[]{:S(2)}) collective-permute-start(bf16[544,128]{1,0:T(8,128)(2,1)S(1)} %concatenate.6), channel_id=1, source_target_pairs={{0,2},{1,3},{2,4},{3,5},{4,6},{5,7},{6,0},{7,1},{8,10},{9,11},{10,... | collective-permute-start | bytes 417800 | tf_op jit(solution)/shard_map/ppermute | solution.py:37
  15.3 9.6 %collective-permute-start.1 = (bf16[544,128]{1,0:T(8,128)(2,1)S(1)}, bf16[544,128]{1,0:T(8,128)(2,1)S(1)}, u32[]{:S(2)}, u32[]{:S(2)}) collective-permute-start(bf16[544,128]{1,0:T(8,128)(2,1)S(1)} %concatenate.6), channel_id=1, source_target_pairs={{0,6},{1,7},{2,0},{3,1},{4,2},{5,3},{6,4},{7,5},{8,14},{9,15},{10,... | collective-permute-start | bytes 417800 | tf_op jit(solution)/shard_map/ppermute | solution.py:37
  16.8 8.4 %collective-permute-start.2 = (bf16[544,128]{1,0:T(8,128)(2,1)S(1)}, bf16[544,128]{1,0:T(8,128)(2,1)S(1)}, u32[]{:S(2)}, u32[]{:S(2)}) collective-permute-start(bf16[544,128]{1,0:T(8,128)(2,1)S(1)} %concatenate.6), channel_id=1, source_target_pairs={{0,4},{1,5},{2,6},{3,7},{4,0},{5,1},{6,2},{7,3},{8,12},{9,13},{10,... | collective-permute-start | bytes 417800 | tf_op jit(solution)/shard_map/ppermute | solution.py:37
  18.9 7.5 %collective-permute-start.3 = (bf16[544,128]{1,0:T(8,128)(2,1)S(1)}, bf16[544,128]{1,0:T(8,128)(2,1)S(1)}, u32[]{:S(2)}, u32[]{:S(2)}) collective-permute-start(bf16[544,128]{1,0:T(8,128)(2,1)S(1)} %concatenate.7), channel_id=1, source_target_pairs={{0,8},{1,9},{2,10},{3,11},{4,12},{5,13},{6,14},{7,15},{8,16},{9,17... | collective-permute-start | bytes 417800 | tf_op jit(solution)/shard_map/ppermute | solution.py:37
  20.8 7.9 %collective-permute-start.4 = (bf16[544,128]{1,0:T(8,128)(2,1)S(1)}, bf16[544,128]{1,0:T(8,128)(2,1)S(1)}, u32[]{:S(2)}, u32[]{:S(2)}) collective-permute-start(bf16[544,128]{1,0:T(8,128)(2,1)S(1)} %concatenate.7), channel_id=1, source_target_pairs={{0,24},{1,25},{2,26},{3,27},{4,28},{5,29},{6,30},{7,31},{8,0},{9,1... | collective-permute-start | bytes 417800 | tf_op jit(solution)/shard_map/ppermute | solution.py:37
  23.0 7.6 %collective-permute-start.5 = (bf16[544,128]{1,0:T(8,128)(2,1)S(1)}, bf16[544,128]{1,0:T(8,128)(2,1)S(1)}, u32[]{:S(2)}, u32[]{:S(2)}) collective-permute-start(bf16[544,128]{1,0:T(8,128)(2,1)S(1)} %concatenate.7), channel_id=1, source_target_pairs={{0,16},{1,17},{2,18},{3,19},{4,20},{5,21},{6,22},{7,23},{8,24},{9,... | collective-permute-start | bytes 417800 | tf_op jit(solution)/shard_map/ppermute | solution.py:37
  31.5 22.6 %collective-permute-start.10 = (bf16[4,544,128]{2,1,0:T(8,128)(2,1)}, bf16[4,544,128]{2,1,0:T(8,128)(2,1)}, u32[]{:S(2)}, u32[]{:S(2)}) collective-permute-start(bf16[4,544,128]{2,1,0:T(8,128)(2,1)} %pad_maximum_fusion.1.refs_2_), channel_id=1, source_target_pairs={{0,6},{1,7},{2,0},{3,1},{4,2},{5,3},{6,4},{7,5},{8,14},{9,15},{10,... | collective-permute-start | bytes 1671176 | tf_op jit(solution)/shard_map/ppermute | solution.py:37
  32.5 21.6 %collective-permute-start.8 = (bf16[4,544,128]{2,1,0:T(8,128)(2,1)}, bf16[4,544,128]{2,1,0:T(8,128)(2,1)}, u32[]{:S(2)}, u32[]{:S(2)}) collective-permute-start(bf16[4,544,128]{2,1,0:T(8,128)(2,1)} %pad_maximum_fusion.1.refs_2_), channel_id=1, source_target_pairs={{0,2},{1,3},{2,4},{3,5},{4,6},{5,7},{6,0},{7,1},{8,10},{9,11},{10,... | collective-permute-start | bytes 1671176 | tf_op jit(solution)/shard_map/ppermute | solution.py:37
  34.4 19.8 %collective-permute-start.7 = (bf16[4,544,128]{2,1,0:T(8,128)(2,1)}, bf16[4,544,128]{2,1,0:T(8,128)(2,1)}, u32[]{:S(2)}, u32[]{:S(2)}) collective-permute-start(bf16[4,544,128]{2,1,0:T(8,128)(2,1)} %pad_maximum_fusion.refs_1_), channel_id=1, source_target_pairs={{0,8},{1,9},{2,10},{3,11},{4,12},{5,13},{6,14},{7,15},{8,16},{9,17... | collective-permute-start | bytes 1671176 | tf_op jit(solution)/shard_map/ppermute | solution.py:37
  35.5 18.6 %collective-permute-start.9 = (bf16[4,544,128]{2,1,0:T(8,128)(2,1)}, bf16[4,544,128]{2,1,0:T(8,128)(2,1)}, u32[]{:S(2)}, u32[]{:S(2)}) collective-permute-start(bf16[4,544,128]{2,1,0:T(8,128)(2,1)} %pad_maximum_fusion.refs_1_), channel_id=1, source_target_pairs={{0,24},{1,25},{2,26},{3,27},{4,28},{5,29},{6,30},{7,31},{8,0},{9,1... | collective-permute-start | bytes 1671176 | tf_op jit(solution)/shard_map/ppermute | solution.py:37
  39.1 19.8 %copy-start.1 = (bf16[8,512,128]{2,1,0:T(8,128)(2,1)S(1)}, bf16[8,512,128]{2,1,0:T(8,128)(2,1)}, u32[]{:S(2)}) copy-start(bf16[8,512,128]{2,1,0:T(8,128)(2,1)} %all-gather.3.cloned.1.call-done.refs_3_.refs_5_) | copy-start | bytes 3145732
  54.2 18.6 %collective-permute-start.11 = (bf16[4,544,128]{2,1,0:T(8,128)(2,1)}, bf16[4,544,128]{2,1,0:T(8,128)(2,1)S(1)}, u32[]{:S(2)}, u32[]{:S(2)}) collective-permute-start(bf16[4,544,128]{2,1,0:T(8,128)(2,1)} %pad_maximum_fusion.refs_1_), channel_id=1, source_target_pairs={{0,16},{1,17},{2,18},{3,19},{4,20},{5,21},{6,22},{7,23},{8,24},{9,... | collective-permute-start | bytes 1671176 | tf_op jit(solution)/shard_map/ppermute | solution.py:37
  56.9 15.9 %collective-permute-start.12 = (bf16[4,544,128]{2,1,0:T(8,128)(2,1)}, bf16[4,544,128]{2,1,0:T(8,128)(2,1)S(1)}, u32[]{:S(2)}, u32[]{:S(2)}) collective-permute-start(bf16[4,544,128]{2,1,0:T(8,128)(2,1)} %pad_maximum_fusion.1.refs_2_), channel_id=1, source_target_pairs={{0,4},{1,5},{2,6},{3,7},{4,0},{5,1},{6,2},{7,3},{8,12},{9,13},{10,... | collective-permute-start | bytes 1671176 | tf_op jit(solution)/shard_map/ppermute | solution.py:37
  83.6 14.1 %collective-permute-start.16 = (f32[4,512,128]{2,1,0:T(8,128)S(1)}, f32[4,512,128]{2,1,0:T(8,128)S(1)}, u32[]{:S(2)}, u32[]{:S(2)}) collective-permute-start(f32[4,512,128]{2,1,0:T(8,128)S(1)} %slice_add_fusion), channel_id=1, source_target_pairs={{0,1},{1,0},{2,3},{3,2},{4,5},{5,4},{6,7},{7,6},{8,9},{9,8},{10,11... | collective-permute-start | bytes 3145736 | tf_op jit(solution)/shard_map/ppermute | solution.py:37
  84.5 1.8 %collective-permute-start.13 = (f32[4,2,512]{2,1,0:T(2,128)S(1)}, f32[4,2,512]{2,1,0:T(2,128)S(1)}, u32[]{:S(2)}, u32[]{:S(2)}) collective-permute-start(f32[4,2,512]{2,1,0:T(2,128)S(1)} %select_add_fusion), channel_id=1, source_target_pairs={{0,1},{1,0},{2,3},{3,2},{4,5},{5,4},{6,7},{7,6},{8,9},{9,8},{10,11... | collective-permute-start | bytes 49160 | tf_op jit(solution)/shard_map/ppermute | solution.py:37
  86.6 5.7 %collective-permute-start.14 = (f32[4,2,512]{2,1,0:T(2,128)S(1)}, f32[4,2,512]{2,1,0:T(2,128)S(1)}, u32[]{:S(2)}, u32[]{:S(2)}) collective-permute-start(f32[4,2,512]{2,1,0:T(2,128)S(1)} %fusion.18), channel_id=1, source_target_pairs={{0,32},{32,0},{64,96},{96,64},{1,33},{33,1},{65,97},{97,65},{2,34}... | collective-permute-start | bytes 49160 | tf_op jit(solution)/shard_map/ppermute | solution.py:45
  92.3 5.3 %collective-permute-start.15 = (f32[4,2,512]{2,1,0:T(2,128)S(1)}, f32[4,2,512]{2,1,0:T(2,128)S(1)}, u32[]{:S(2)}, u32[]{:S(2)}) collective-permute-start(f32[4,2,512]{2,1,0:T(2,128)S(1)} %add.121), channel_id=1, source_target_pairs={{0,64},{32,96},{64,0},{96,32},{1,65},{33,97},{65,1},{97,33},{2,66}... | collective-permute-start | bytes 49160 | tf_op jit(solution)/shard_map/ppermute | solution.py:45
  101.2 13.5 %collective-permute-start.17 = (f32[512,128]{1,0:T(8,128)}, f32[512,128]{1,0:T(8,128)}, u32[]{:S(2)}, u32[]{:S(2)}) collective-permute-start(f32[512,128]{1,0:T(8,128)} %get-tuple-element.73), channel_id=1, source_target_pairs={{0,32},{32,64},{64,96},{96,0},{1,33},{33,65},{65,97},{97,1},{2,34}... | collective-permute-start | bytes 786440 | tf_op jit(solution)/shard_map/ppermute | solution.py:41
  103.2 11.5 %collective-permute-start.18 = (f32[512,128]{1,0:T(8,128)}, f32[512,128]{1,0:T(8,128)}, u32[]{:S(2)}, u32[]{:S(2)}) collective-permute-start(f32[512,128]{1,0:T(8,128)} %get-tuple-element.75), channel_id=1, source_target_pairs={{0,64},{32,96},{64,0},{96,32},{1,65},{33,97},{65,1},{97,33},{2,66}... | collective-permute-start | bytes 786440 | tf_op jit(solution)/shard_map/ppermute | solution.py:41
  103.8 11.5 %collective-permute-start.19 = (f32[512,128]{1,0:T(8,128)S(1)}, f32[512,128]{1,0:T(8,128)}, u32[]{:S(2)}, u32[]{:S(2)}) collective-permute-start(f32[512,128]{1,0:T(8,128)S(1)} %get-tuple-element.74), channel_id=1, source_target_pairs={{0,96},{32,0},{64,32},{96,64},{1,97},{33,1},{65,33},{97,65},{2,98}... | collective-permute-start | bytes 786440 | tf_op jit(solution)/shard_map/ppermute | solution.py:41
  106.8 23.0 %copy-start.7 = (bf16[1024]{0:T(1024)(128)(2,1)S(1)}, bf16[1024]{0:T(1024)(128)(2,1)}, u32[]{:S(2)}) copy-start(bf16[1024]{0:T(1024)(128)(2,1)} %param.7) | copy-start | bytes 6148
  116.4 13.4 %all-to-all-start = ((f32[16,8,128]{2,1,0:T(8,128)}), f32[16,8,128]{2,1,0:T(8,128)S(1)}, u32[]{:S(2)}, u32[]{:S(2)}) async-start(f32[16,8,128]{2,1,0:T(8,128)} %bitcast.22), calls=%async_computation | async-start | bytes 131072 | tf_op jit(solution)/shard_map/all_to_all | solution.py:379
  (6 other events, 15.6 us)
Sparse Core Ops, SparseCore 0:
  11.3 26.5 all-gather.2

commit v3 on v2

--- a/solution.py
+++ b/solution.py
@@ -16,7 +16,7 @@
 META = HB * PBS
 ROWS = META + 32
 TABLE = 152
-LOW = 76
+LOW = 100
 RING = 8
 DUMMY = 8
 NONE = 128
@@ -45,7 +45,52 @@
     return lax.ppermute(v, "gx", [(i, i ^ s) for i in range(4)])
 
 
-def pair_kernel(steps, before, *refs):
+def prep_kernel(ids_ref, lens_ref, part_ref, weight_ref, out0_ref, out1_ref, rows):
+    ones = jnp.ones((8, 128), bf16)
+    lanes = lax.broadcasted_iota(jnp.int32, (8, 128), 1)
+    weights = weight_ref[...].astype(f32)
+    for h, out_ref in enumerate((out0_ref, out1_ref)):
+        out_ref[0:META, :] = part_ref[h * META:(h + 1) * META, :]
+        gate = jnp.zeros((8, 128), jnp.int32)
+        for j in range(HB):
+            b = h * HB + j
+            block = part_ref[b * PBS:(b + 1) * PBS, :].astype(f32)
+            square = block * block
+            hi = square.astype(bf16)
+            lo = (square - hi.astype(f32)).astype(bf16)
+            total = sum(
+                lax.dot_general(ones, v, (((1,), (1,)), ((), ())), preferred_element_type=f32) for v in (hi, lo)
+            )
+            total = total[0:1] * (-0.5 * SCALE)
+            rows[j:j + 1, :] = weights[b:b + 1]
+            for k in range(1, 4):
+                piece = total.astype(bf16).astype(f32)
+                rows[k * HB + j:k * HB + j + 1, :] = piece
+                total = total - piece
+            for g in range(16):
+                d = ids_ref[b, g]
+                at = jnp.where(g < lens_ref[b], (d % 32) // 2 * HB + j, -1)
+                gate = gate + jnp.where(lanes == at, 1 << (d // 32 * 2 + d % 2), 0)
+        out_ref[META:META + 16, :] = rows[...].astype(bf16)
+        gate = gate.astype(f32)
+        out_ref[META + 16:META + 32, :] = jnp.concatenate([gate, gate], axis=0).astype(bf16)
+
+
+def prep_call(particles, weights, gate_ids, gate_lens):
+    vm = pl.BlockSpec(memory_space=pltpu.VMEM)
+    sm = pl.BlockSpec(memory_space=pltpu.SMEM)
+    half = jax.ShapeDtypeStruct((ROWS, 128), bf16)
+    return pl.pallas_call(
+        prep_kernel,
+        out_shape=(half, half),
+        in_specs=[sm, sm, vm, vm],
+        out_specs=(vm, vm),
+        scratch_shapes=[pltpu.VMEM((16, 128), f32)],
+        name="payload",
+    )(gate_ids, gate_lens, particles, weights.reshape(8, PBS))
+
+
+def pair_kernel(steps, before, last, *refs):
     parts = 2 * len(steps)
     count = parts * 16
     pos_ref, refs = refs[0], refs[1:]
@@ -54,8 +99,14 @@
     first = before == 0
     tables, refs = refs[:before], refs[before:]
     if not first:
-        as_ref, refs = refs[0], refs[2:]
-    mom_ref, mass_ref, low_ref, slot_ref, refs = refs[0], refs[1], refs[2], refs[3], refs[4:]
+        mom_in, mass_in, as_ref, refs = refs[0], refs[1], refs[2], refs[4:]
+    if last:
+        near_ref, far_ref = refs[:2]
+        mom_ref, done = refs[-2:]
+        refs = refs[2:-2]
+    else:
+        mom_ref, refs = refs[0], refs[1:]
+    mass_ref, low_ref, slot_ref, refs = refs[0], refs[1], refs[2], refs[3:]
     if first:
         as_ref, refs = refs[0], refs[1:]
     lst, gates, grow, meta, xs, wrow, brow, cr0, cr1, w0, w1, ring, sem, xsem, msem = refs
@@ -72,14 +123,17 @@
     ]
     for copy in heads + loads:
         copy.start()
-    mom_ref[...] = jnp.zeros_like(mom_ref)
-    mass_ref[...] = jnp.zeros_like(mass_ref)
     if first:
+        mom_ref[...] = jnp.zeros_like(mom_ref)
+        mass_ref[...] = jnp.zeros_like(mass_ref)
         for r in range(8):
             for h in range(0, DBS, 128):
                 d = det_ref[r, h:h + 128, :].astype(f32)
                 v = jnp.sum(d * d, axis=1, keepdims=True) * (-0.5 * SCALE) + 16.0 * LOG2E
                 as_ref[r, h:h + 128, :] = jnp.broadcast_to(v, (128, 128))
+    else:
+        mom_ref[...] = mom_in[...]
+        mass_ref[...] = mass_in[...]
     base = jnp.int32(0)
     for table in tables:
         base = base + (table[3, 0] + 1) // 2
@@ -96,7 +150,6 @@
     wrow[count:count + 8, :] = jnp.zeros((8, 128), f32)
     gate_load.wait()
 
-    bits = [r ^ c for r in range(8)]
     counts = [jnp.int32(0)] * 8
     for s in range(parts * 4):
         h, step, u = s // 4 % 2, steps[s // 8], s % 4
@@ -107,7 +160,7 @@
             v = (home + j) * 256 + (s * 4 + j)
             for r in range(8):
                 lst[r, counts[r]] = v
-                counts[r] = counts[r] + ((m >> bits[r]) & 1)
+                counts[r] = counts[r] + ((m >> r) & 1)
 
     def put(q, v0, v1, r):
         slot_ref[0, q] = v0
@@ -163,8 +216,7 @@
             w[s][rows, :] = wtd.astype(bf16)
 
     def moment(q, s):
-        r = slot_ref[2, q]
-        mom_ref[jnp.where(r < DUMMY, r // 2 + r % 2 * 4, DUMMY)] += jnp.dot(w[s][...], both(q), preferred_element_type=f32)
+        mom_ref[slot_ref[2, q]] += jnp.dot(w[s][...], both(q), preferred_element_type=f32)
 
     cross(1, 1)
 
@@ -192,30 +244,45 @@
         copy_out(0, j).wait()
         return carry
 
+    if last:
+        out = [
+            pltpu.make_async_copy(mom_ref.at[2 * k + (c ^ d)], (near_ref, far_ref)[d].at[k], done.at[2 * k + d])
+            for d in (1, 0)
+            for k in range(4)
+        ]
+        for copy in out:
+            copy.start()
     lax.fori_loop(0, jnp.minimum(total, RING), drain, 0)
-
-
-def pair_call(steps, pos, parts, dets, tables, state):
+    if last:
+        for copy in out:
+            copy.wait()
+
+
+def pair_call(steps, last, pos, parts, dets, tables, state):
     n = len(parts)
     first = state is None
     vm = pl.BlockSpec(memory_space=pltpu.VMEM)
     sm = pl.BlockSpec(memory_space=pltpu.SMEM)
     hb = pl.BlockSpec(memory_space=pl.ANY)
     acc = jax.ShapeDtypeStruct((9, DBS, 128), f32)
+    half = jax.ShapeDtypeStruct((4, DBS, 128), f32)
     low = jax.ShapeDtypeStruct((LOW, 2, DBS, 256), bf16)
     table = jax.ShapeDtypeStruct((4, TABLE), jnp.int32)
     operands, specs = [pos] + parts + [dets], [sm] + [hb] * n + [vm]
     outs, out_specs = [acc, acc, low, table], [vm, vm, hb, sm]
-    aliases = {}
+    aliases, extra = {}, []
     if first:
         outs, out_specs = outs + [jax.ShapeDtypeStruct((8, DBS, 128), f32)], out_specs + [vm]
     else:
         operands += tables + list(state)
-        specs += [sm] * len(tables) + [vm, hb]
-        aliases = {len(specs) - 1: 2}
+        specs += [sm] * len(tables) + [vm, vm, vm, hb]
+        aliases = {len(specs) - 1: 2 + last}
+    if last:
+        outs, out_specs = [half, half] + outs[1:], [hb, hb] + out_specs[1:]
+        extra = [pltpu.VMEM((9, DBS, 128), f32), pltpu.SemaphoreType.DMA((8,))]
     work = 26 * n // 2
     return pl.pallas_call(
-        functools.partial(pair_kernel, steps, len(tables)),
+        functools.partial(pair_kernel, steps, len(tables), last),
         out_shape=outs,
         in_specs=specs,
         out_specs=out_specs,
@@ -235,7 +302,7 @@
             pltpu.SemaphoreType.DMA((RING,)),
             pltpu.SemaphoreType.DMA((n,)),
             pltpu.SemaphoreType.DMA((n,)),
-        ],
+        ] + extra,
         input_output_aliases=aliases,
         compiler_params=pltpu.CompilerParams(vmem_limit_bytes=14 << 20),
         cost_estimate=pl.CostEstimate(
@@ -307,7 +374,7 @@
             pltpu.VMEM((RING, 2, DBS, 256), bf16),
             pltpu.SemaphoreType.DMA((RING,)),
         ],
-        compiler_params=pltpu.CompilerParams(vmem_limit_bytes=30 << 20),
+        compiler_params=pltpu.CompilerParams(vmem_limit_bytes=14 << 20),
         cost_estimate=pl.CostEstimate(flops=104 * DBS * PBS * 2, transcendentals=0, bytes_accessed=104 * DBS * PBS * 2),
         name="shares",
     )(*tables, inv_b, low)
@@ -318,30 +385,10 @@
     c, alpha = gy % 2, gy // 2
     pos = jnp.stack([c, gy // 8, gy // 2 % 4]).astype(jnp.int32)
 
-    half = jnp.sum(jnp.square(particles.astype(f32)), axis=1).reshape(8, PBS) * (-0.5 * SCALE)
-    hi = lax.reduce_precision(half, 8, 7)
-    mid = lax.reduce_precision(half - hi, 8, 7)
-    lo = (half - hi) - mid
-    live = jnp.arange(16, dtype=jnp.int32)[None, :] < gate_lens[:, None]
-    bit = jnp.where(live, 1 << ((gate_ids // 32) * 2 + gate_ids % 2), 0)
-    owner = (gate_ids % 32) // 2
-    masks = jnp.sum(jnp.where(owner[:, None, :] == jnp.arange(16)[None, :, None], bit[:, None, :], 0), axis=2)
-    rows = [weights.reshape(8, PBS), hi.astype(bf16), mid.astype(bf16), lo.astype(bf16)]
-    sends = []
-    for h in range(2):
-        own = slice(h * HB, (h + 1) * HB)
-        gate = jnp.transpose(masks[own]).reshape(1, 64).astype(bf16)
-        sends.append(
-            jnp.concatenate(
-                [particles[h * META:(h + 1) * META]]
-                + [v[own] for v in rows]
-                + [jnp.pad(gate, ((0, 15), (0, 64)))]
-            )
-        )
-
-    dets = lax.all_gather(jnp.stack([detections, gy_shift(detections, 0, 0, 1)]), "gx").reshape(8, DBS, 128)
-
-    sends = lax.optimization_barrier(sends)
+    groups = [[x * 32 + a * 2 + d for x in range(4) for d in range(2)] for a in range(16)]
+    dets = lax.all_gather(detections, ("gx", "gy"), axis_index_groups=groups)
+
+    sends = prep_call(particles, weights, gate_ids, gate_lens)
     first = [
         [sends[0]] + [gy_shift(sends[0], 0, s) for s in (1, 3, 2)],
         [sends[1]] + [gy_shift(sends[1], s, 0) for s in (1, 3, 2)],
@@ -350,29 +397,27 @@
     halves = [jnp.stack([v[0], v[1], v[3], v[2]]) for v in first]
 
     second = [v for s in (1, 3) for v in (gy_shift(halves[0], s, 0), gy_shift(halves[1], 0, s))]
-    mom1, mass1, low, ta, as_b = pair_call((0,), pos, halves, dets, [], None)
-    sum1 = jnp.sum(mass1, axis=2)
-    second, halves, sum1 = lax.optimization_barrier((second, halves, sum1))
+    mom, mass, low, ta, as_b = pair_call((0,), False, pos, halves, dets, [], None)
+    second, halves, ta = lax.optimization_barrier((second, halves, ta))
     third = [gy_shift(halves[0], 2, 0), gy_shift(halves[1], 0, 2)]
-    mom2, mass2, low, tb = pair_call((1, 3), pos, second, dets, [ta], (as_b, low))
-    mom3, mass3, low, tc = pair_call((2,), pos, third, dets, [ta, tb], (as_b, low))
-
-    part = (sum1 + jnp.sum(mass2 + mass3, axis=2))[:8].reshape(4, 2, DBS) * DETECT_PROB
-    mine = (jnp.arange(4)[:, None, None] == gx) & (jnp.arange(2)[None, :, None] == 0)
+    mom, mass, low, tb = pair_call((1, 3), False, pos, second, dets, [ta], (mom, mass, as_b, low))
+    near, far, mass, low, tc = pair_call((2,), True, pos, third, dets, [ta, tb], (mom, mass, as_b, low))
+
+    part = jnp.sum(mass, axis=2)[:8].reshape(4, 2, DBS) * DETECT_PROB
+    mine = (jnp.arange(4)[:, None, None] == gx) & (jnp.arange(2)[None, :, None] == c)
     part = part + jnp.where(mine, clutter[None, None, :], 0.0)
-    norm = part + gy_shift(part, 0, 0, 1)[:, ::-1]
+    norm = part + gy_shift(part, 0, 0, 1)
     norm = norm + x_swap(norm, 1)
+    own = near + gy_shift(far, 0, 0, 1)
+    norm, own = lax.optimization_barrier((norm, own))
     norm = norm + x_swap(norm, 2)
     inv = (1.0 / norm).astype(bf16).astype(f32)
     inv_b = jnp.broadcast_to(inv.reshape(8, DBS)[:, :, None], (8, DBS, 128))
 
-    far = mom1[4:8] + mom2[4:8] + mom3[4:8]
-    own = mom1[0:4] + mom2[0:4] + mom3[0:4] + gy_shift(far, 0, 0, 1)
-    inv_b, own = lax.optimization_barrier((inv_b, own))
     moment = lax.dynamic_index_in_dim(own, gx, 0, False)
     for s in (1, 2, 3):
         moment = moment + x_shift(lax.dynamic_index_in_dim(own, (gx + s) % 4, 0, False), s)
-    normalizer = lax.dynamic_index_in_dim(norm[:, 0], gx, 0, False)
+    normalizer = lax.dynamic_index_in_dim(norm.reshape(8, DBS), gx * 2 + c, 0, False)
 
     share = share_call((ta, tb, tc), inv_b, low)
     share, moment = lax.optimization_barrier((share, moment))

time: 137 us -> 121 us (0.88)
  other arithmetic: 15.8 us -> 5.83 us
  local copies, waits for them, and re-layouts: 8.7 us -> 2.53 us
  starting transfers between devices: 39.2 us -> 36.8 us
    ppermute x2, starting transfers between devices: 6.48 us -> 1.75 us  [x_swap(): return lax.ppermute(v, 'gx', [(i, i ^ s) for i in range(4)])]
    reduce_sum x4 -> x1, other arithmetic: 4.41 us -> 0.68 us  [local(): part = jnp.sum(mass, axis=2)[:8].reshape(4, 2, DBS) * DETECT_PROB]
    add x3 -> x2, other arithmetic: 4.35 us -> 1.41 us  [the longest x1 1.33 us: local(): own = near + gy_shift(far, 0, 0, 1)]
    unnamed x16 -> x8, local copies, waits for them, and re-layouts: 4.11 us -> 1.24 us
    ppermute x15 -> x14, starting transfers between devices: 22 us -> 24.7 us  [gy_shift(): return lax.ppermute(v, 'gy', perm)]
    slice x5 -> x0, local copies, waits for them, and re-layouts: 1.78 us -> none  [the longest x1 0.99 us: local(): particles[h * META:(h + 1) * META]]
    another operation x2 -> x0, other arithmetic: 1.64 us -> none  [the longest x1 1.63 us: local(): jnp.stack([detections, gy_shift(detections, 0, 0, 1)])]
    ppermute x15 -> x14, waiting for transfers between devices: 7.02 us -> 8.06 us  [gy_shift(): return lax.ppermute(v, 'gy', perm)]
  transfers between devices with their start and end apart: 22 -> 21, of which waited for: 11 -> 10; matrix products, arithmetic and copies ran while one was open for 8% -> 4% of each run, Pallas kernels for 23% -> 26%
where the time goes in v3:
time: 121 us; the launch traced here: 120 us
  Pallas kernels  39.9 us (33%)
  starting transfers between devices  36.8 us (30%)
  waiting for transfers between devices  20.6 us (17%)
  between operations  14.3 us (12%)
  other arithmetic  5.83 us (5%)
  local copies, waits for them, and re-layouts  2.53 us (2%)
    pallas_call x3, Pallas kernels, pair_call(): pl.pallas_call(functools.partial(pair_kernel, steps, len(tables), last),...  29.3 us
    ppermute x14, starting transfers between devices, gy_shift(): return lax.ppermute(v, 'gy', perm)  24.7 us
    ppermute x14, waiting for transfers between devices, gy_shift(): return lax.ppermute(v, 'gy', perm)  8.06 us
    pallas_call x1, Pallas kernels, share_call(): pl.pallas_call(share_kernel, out_shape=jax.ShapeDtypeStruct((NONE, 128),...  7.13 us
    all_to_all x1, waiting for transfers between devices, local(): lax.all_to_all(share.reshape(16, 8, 128), 'gy', split_axis=0, concat_axis...  6.82 us
    all_to_all x1, starting transfers between devices, local(): lax.all_to_all(share.reshape(16, 8, 128), 'gy', split_axis=0, concat_axis...  5.64 us
    ppermute x3, starting transfers between devices, x_shift(): return lax.ppermute(v, 'gx', [(i, (i + s) % 4) for i in range(4)])  4.65 us
    ppermute x2, waiting for transfers between devices, x_swap(): return lax.ppermute(v, 'gx', [(i, i ^ s) for i in range(4)])  3.68 us
  transfers between devices with their start and end apart: 21, of which 10 were waited for; matrix products, arithmetic and copies ran while one was open for 4% of the time, Pallas kernels for 26%

profile of v3, /device:TPU:0, one launch (start us, length us, event | category | flops | bytes accessed | tf_op | source)
XLA Modules:
  0.0 119.9 jit_solution(5342876622880256800)
XLA Ops:
  7.9 3.4 %payload.1 = (bf16[544,128]{1,0:T(8,128)(2,1)}, bf16[544,128]{1,0:T(8,128)(2,1)}) custom-call(s32[8,16]{1,0:T(8,128)} %ids_ref.1, s32[8]{0:T(128)} %lens_ref.1, bf16[1024,128]{1,0:T(8,128)(2,1)} %part_ref.1, bf16[8,128]{1,0:T(8,128)(2,1)} %bitcast.42), custom_call_target="tpu_custom_call" | custom-call | tf_op jit(solution)/shard_map/payload/pallas_call | solution.py:83
  11.3 1.7 %collective-permute-start = (bf16[544,128]{1,0:T(8,128)(2,1)}, bf16[544,128]{1,0:T(8,128)(2,1)S(1)}, u32[]{:S(2)}, u32[]{:S(2)}) collective-permute-start(bf16[544,128]{1,0:T(8,128)(2,1)} %get-tuple-element.40), channel_id=1, source_target_pairs={{0,2},{1,3},{2,4},{3,5},{4,6},{5,7},{6,0},{7,1},{8,10},{9,11},{10,... | collective-permute-start | bytes 417800 | tf_op jit(solution)/shard_map/ppermute | solution.py:37
  13.0 1.6 %collective-permute-start.1 = (bf16[544,128]{1,0:T(8,128)(2,1)}, bf16[544,128]{1,0:T(8,128)(2,1)S(1)}, u32[]{:S(2)}, u32[]{:S(2)}) collective-permute-start(bf16[544,128]{1,0:T(8,128)(2,1)} %get-tuple-element.40), channel_id=1, source_target_pairs={{0,6},{1,7},{2,0},{3,1},{4,2},{5,3},{6,4},{7,5},{8,14},{9,15},{10,... | collective-permute-start | bytes 417800 | tf_op jit(solution)/shard_map/ppermute | solution.py:37
  14.5 2.1 %collective-permute-start.2 = (bf16[544,128]{1,0:T(8,128)(2,1)}, bf16[544,128]{1,0:T(8,128)(2,1)S(1)}, u32[]{:S(2)}, u32[]{:S(2)}) collective-permute-start(bf16[544,128]{1,0:T(8,128)(2,1)} %get-tuple-element.40), channel_id=1, source_target_pairs={{0,4},{1,5},{2,6},{3,7},{4,0},{5,1},{6,2},{7,3},{8,12},{9,13},{10,... | collective-permute-start | bytes 417800 | tf_op jit(solution)/shard_map/ppermute | solution.py:37
  16.6 1.9 %collective-permute-start.3 = (bf16[544,128]{1,0:T(8,128)(2,1)}, bf16[544,128]{1,0:T(8,128)(2,1)S(1)}, u32[]{:S(2)}, u32[]{:S(2)}) collective-permute-start(bf16[544,128]{1,0:T(8,128)(2,1)} %get-tuple-element.44), channel_id=1, source_target_pairs={{0,8},{1,9},{2,10},{3,11},{4,12},{5,13},{6,14},{7,15},{8,16},{9,17... | collective-permute-start | bytes 417800 | tf_op jit(solution)/shard_map/ppermute | solution.py:37
  18.5 2.1 %collective-permute-start.4 = (bf16[544,128]{1,0:T(8,128)(2,1)}, bf16[544,128]{1,0:T(8,128)(2,1)S(1)}, u32[]{:S(2)}, u32[]{:S(2)}) collective-permute-start(bf16[544,128]{1,0:T(8,128)(2,1)} %get-tuple-element.44), channel_id=1, source_target_pairs={{0,24},{1,25},{2,26},{3,27},{4,28},{5,29},{6,30},{7,31},{8,0},{9,1... | collective-permute-start | bytes 417800 | tf_op jit(solution)/shard_map/ppermute | solution.py:37
  20.6 1.9 %collective-permute-start.5 = (bf16[544,128]{1,0:T(8,128)(2,1)}, bf16[544,128]{1,0:T(8,128)(2,1)S(1)}, u32[]{:S(2)}, u32[]{:S(2)}) collective-permute-start(bf16[544,128]{1,0:T(8,128)(2,1)} %get-tuple-element.44), channel_id=1, source_target_pairs={{0,16},{1,17},{2,18},{3,19},{4,20},{5,21},{6,22},{7,23},{8,24},{9,... | collective-permute-start | bytes 417800 | tf_op jit(solution)/shard_map/ppermute | solution.py:37
  22.5 1.8 %collective-permute-done.3 = bf16[544,128]{1,0:T(8,128)(2,1)S(1)} collective-permute-done((bf16[544,128]{1,0:T(8,128)(2,1)}, bf16[544,128]{1,0:T(8,128)(2,1)S(1)}, u32[]{:S(2)}, u32[]{:S(2)}) %collective-permute-start.3) | collective-permute-done | bytes 139296 | tf_op jit(solution)/shard_map/ppermute | solution.py:37
  24.3 2.3 %collective-permute-done.4 = bf16[544,128]{1,0:T(8,128)(2,1)S(1)} collective-permute-done((bf16[544,128]{1,0:T(8,128)(2,1)}, bf16[544,128]{1,0:T(8,128)(2,1)S(1)}, u32[]{:S(2)}, u32[]{:S(2)}) %collective-permute-start.4) | collective-permute-done | bytes 139296 | tf_op jit(solution)/shard_map/ppermute | solution.py:37
  26.6 1.6 %collective-permute-done.5 = bf16[544,128]{1,0:T(8,128)(2,1)S(1)} collective-permute-done((bf16[544,128]{1,0:T(8,128)(2,1)}, bf16[544,128]{1,0:T(8,128)(2,1)S(1)}, u32[]{:S(2)}, u32[]{:S(2)}) %collective-permute-start.5) | collective-permute-done | bytes 139296 | tf_op jit(solution)/shard_map/ppermute | solution.py:37
  29.9 2.6 %collective-permute-start.9 = (bf16[4,544,128]{2,1,0:T(8,128)(2,1)S(1)}, bf16[4,544,128]{2,1,0:T(8,128)(2,1)S(1)}, u32[]{:S(2)}, u32[]{:S(2)}) collective-permute-start(bf16[4,544,128]{2,1,0:T(8,128)(2,1)S(1)} %pad_maximum_fusion.1.refs_2_), channel_id=1, source_target_pairs={{0,6},{1,7},{2,0},{3,1},{4,2},{5,3},{6,4},{7,5},{8,14},{9,15},{10,... | collective-permute-start | bytes 1671176 | tf_op jit(solution)/shard_map/ppermute | solution.py:37
  34.3 2.4 %collective-permute-start.8 = (bf16[4,544,128]{2,1,0:T(8,128)(2,1)S(1)}, bf16[4,544,128]{2,1,0:T(8,128)(2,1)S(1)}, u32[]{:S(2)}, u32[]{:S(2)}) collective-permute-start(bf16[4,544,128]{2,1,0:T(8,128)(2,1)S(1)} %pad_maximum_fusion.refs_1_), channel_id=1, source_target_pairs={{0,24},{1,25},{2,26},{3,27},{4,28},{5,29},{6,30},{7,31},{8,0},{9,1... | collective-permute-start | bytes 1671176 | tf_op jit(solution)/shard_map/ppermute | solution.py:37
  38.0 8.4 %pairs.3 = (f32[9,512,128]{2,1,0:T(8,128)S(1)}, f32[9,512,128]{2,1,0:T(8,128)S(1)}, bf16[100,2,512,256]{3,2,1,0:T(8,128)(2,1)}, s32[4,152]{1,0:T(4,128)S(1)}, f32[8,512,128]{2,1,0:T(8,128)S(1)}) custom-call(s32[3]{0:T(128)S(1)} %pad_add_fusion.refs_0_, bf16[4,544,128]{2,1,0:T(8,128)(2,1)S(1)} %pad_maximum_fusion.refs_1_, ...), custom_call_target="tpu_custom_call" | custom-call | flops 872415232 | bytes 3407872 | tf_op jit(solution)/shard_map/pairs/pallas_call | solution.py:284
  46.9 1.6 %collective-permute-start.10 = (bf16[4,544,128]{2,1,0:T(8,128)(2,1)S(1)}, bf16[4,544,128]{2,1,0:T(8,128)(2,1)S(1)}, u32[]{:S(2)}, u32[]{:S(2)}) collective-permute-start(bf16[4,544,128]{2,1,0:T(8,128)(2,1)S(1)} %pad_maximum_fusion.refs_1_), channel_id=1, source_target_pairs={{0,16},{1,17},{2,18},{3,19},{4,20},{5,21},{6,22},{7,23},{8,24},{9,... | collective-permute-start | bytes 1671176 | tf_op jit(solution)/shard_map/ppermute | solution.py:37
  48.5 4.7 %collective-permute-start.11 = (bf16[4,544,128]{2,1,0:T(8,128)(2,1)S(1)}, bf16[4,544,128]{2,1,0:T(8,128)(2,1)S(1)}, u32[]{:S(2)}, u32[]{:S(2)}) collective-permute-start(bf16[4,544,128]{2,1,0:T(8,128)(2,1)S(1)} %pad_maximum_fusion.1.refs_2_), channel_id=1, source_target_pairs={{0,4},{1,5},{2,6},{3,7},{4,0},{5,1},{6,2},{7,3},{8,12},{9,13},{10,... | collective-permute-start | bytes 1671176 | tf_op jit(solution)/shard_map/ppermute | solution.py:37
  53.2 11.9 %pairs.4 = (f32[9,512,128]{2,1,0:T(8,128)S(1)}, f32[9,512,128]{2,1,0:T(8,128)S(1)}, bf16[100,2,512,256]{3,2,1,0:T(8,128)(2,1)}, s32[4,152]{1,0:T(4,128)S(1)}) custom-call(s32[3]{0:T(128)S(1)} %pad_add_fusion.refs_0_, bf16[4,544,128]{2,1,0:T(8,128)(2,1)S(1)} %collective-permute-done.6.refs_1_, ...), custom_call_target="tpu_custom_call", output_to_operand_aliasing={{2}: (10, {})} | custom-call | flops 1744830464 | bytes 6815744 | tf_op jit(solution)/shard_map/pairs/pallas_call | solution.py:284
  65.9 9.0 %pairs.5 = (f32[4,512,128]{2,1,0:T(8,128)S(1)}, f32[4,512,128]{2,1,0:T(8,128)}, f32[9,512,128]{2,1,0:T(8,128)S(1)}, bf16[100,2,512,256]{3,2,1,0:T(8,128)(2,1)}, s32[4,152]{1,0:T(4,128)S(1)}) custom-call(s32[3]{0:T(128)S(1)} %pad_add_fusion.refs_0_, bf16[4,544,128]{2,1,0:T(8,128)(2,1)S(1)} %collective-permute-done.10.refs_1_, ...), custom_call_target="tpu_custom_call", output_to_operand_aliasing={{3}: (9, {})} | custom-call | flops 872415232 | bytes 3407872 | tf_op jit(solution)/shard_map/pairs/pallas_call | solution.py:284
  77.9 3.7 %collective-permute-done.13 = f32[4,2,512]{2,1,0:T(2,128)S(1)} collective-permute-done((f32[4,2,512]{2,1,0:T(2,128)S(1)}, f32[4,2,512]{2,1,0:T(2,128)S(1)}, u32[]{:S(2)}, u32[]{:S(2)}) %collective-permute-start.13) | collective-permute-done | bytes 16416 | tf_op jit(solution)/shard_map/ppermute | solution.py:45
  82.9 1.7 %collective-permute-start.15 = (f32[4,2,512]{2,1,0:T(2,128)S(1)}, f32[4,2,512]{2,1,0:T(2,128)S(1)}, u32[]{:S(2)}, u32[]{:S(2)}) collective-permute-start(f32[4,2,512]{2,1,0:T(2,128)S(1)} %add.84), channel_id=1, source_target_pairs={{0,64},{32,96},{64,0},{96,32},{1,65},{33,97},{65,1},{97,33},{2,66}... | collective-permute-start | bytes 49160 | tf_op jit(solution)/shard_map/ppermute | solution.py:45
  85.2 2.1 %collective-permute-start.17 = (f32[512,128]{1,0:T(8,128)S(1)}, f32[512,128]{1,0:T(8,128)S(1)}, u32[]{:S(2)}, u32[]{:S(2)}) collective-permute-start(f32[512,128]{1,0:T(8,128)S(1)} %get-tuple-element.77), channel_id=1, source_target_pairs={{0,64},{32,96},{64,0},{96,32},{1,65},{33,97},{65,1},{97,33},{2,66}... | collective-permute-start | bytes 786440 | tf_op jit(solution)/shard_map/ppermute | solution.py:41
  87.3 2.0 %collective-permute-start.18 = (f32[512,128]{1,0:T(8,128)S(1)}, f32[512,128]{1,0:T(8,128)S(1)}, u32[]{:S(2)}, u32[]{:S(2)}) collective-permute-start(f32[512,128]{1,0:T(8,128)S(1)} %get-tuple-element.76), channel_id=1, source_target_pairs={{0,96},{32,0},{64,32},{96,64},{1,97},{33,1},{65,33},{97,65},{2,98}... | collective-permute-start | bytes 786440 | tf_op jit(solution)/shard_map/ppermute | solution.py:41
  90.6 7.1 %shares.1 = f32[128,128]{1,0:T(8,128)} custom-call(s32[4,152]{1,0:T(4,128)S(1)} %get-tuple-element.49.refs_6_.refs_4_.ta, s32[4,152]{1,0:T(4,128)S(1)} %get-tuple-element.58.refs_5_.tb, s32[4,152]{1,0:T(4,128)S(1)} %get-tuple-element.64.tc, f32[8,512,128]{2,1,0:T(8,128)S(1)} %broadcast_in_dim.39.inv_ref, bf16[100,2,512,256]{3,2,1,0:T(8,128)(2,1)} %get-tuple-element.69.low_ref), custom_call_target="tpu_custom_call" | custom-call | flops 13631488 | bytes 13631488 | tf_op jit(solution)/shard_map/shares/pallas_call | solution.py:367
  99.1 5.6 %all-to-all-start = ((f32[16,8,128]{2,1,0:T(8,128)}), f32[16,8,128]{2,1,0:T(8,128)S(1)}, u32[]{:S(2)}, u32[]{:S(2)}) async-start(f32[16,8,128]{2,1,0:T(8,128)} %bitcast.17), calls=%async_computation | async-start | bytes 131072 | tf_op jit(solution)/shard_map/all_to_all | solution.py:424
  105.6 6.8 %all-to-all-done = f32[16,8,128]{2,1,0:T(8,128)S(1)} async-done(((f32[16,8,128]{2,1,0:T(8,128)}), f32[16,8,128]{2,1,0:T(8,128)S(1)}, u32[]{:S(2)}, u32[]{:S(2)}) %all-to-all-start) | async-done | bytes 65568 | tf_op jit(solution)/shard_map/all_to_all | solution.py:424
  (56 shorter events, 15.8 us)
Async XLA Ops:
  7.2 29.6 %all-gather.3.cloned.1.call-start = ((), (), s32[]{:S(2)}) async-start(), calls=%async_computation.1 | async-start | bytes 1179648 | tf_op jit(solution)/shard_map/all_gather | solution.py:389
  11.3 9.3 %collective-permute-start = (bf16[544,128]{1,0:T(8,128)(2,1)}, bf16[544,128]{1,0:T(8,128)(2,1)S(1)}, u32[]{:S(2)}, u32[]{:S(2)}) collective-permute-start(bf16[544,128]{1,0:T(8,128)(2,1)} %get-tuple-element.40), channel_id=1, source_target_pairs={{0,2},{1,3},{2,4},{3,5},{4,6},{5,7},{6,0},{7,1},{8,10},{9,11},{10,... | collective-permute-start | bytes 417800 | tf_op jit(solution)/shard_map/ppermute | solution.py:37
  13.0 9.6 %collective-permute-start.1 = (bf16[544,128]{1,0:T(8,128)(2,1)}, bf16[544,128]{1,0:T(8,128)(2,1)S(1)}, u32[]{:S(2)}, u32[]{:S(2)}) collective-permute-start(bf16[544,128]{1,0:T(8,128)(2,1)} %get-tuple-element.40), channel_id=1, source_target_pairs={{0,6},{1,7},{2,0},{3,1},{4,2},{5,3},{6,4},{7,5},{8,14},{9,15},{10,... | collective-permute-start | bytes 417800 | tf_op jit(solution)/shard_map/ppermute | solution.py:37
  14.5 8.0 %collective-permute-start.2 = (bf16[544,128]{1,0:T(8,128)(2,1)}, bf16[544,128]{1,0:T(8,128)(2,1)S(1)}, u32[]{:S(2)}, u32[]{:S(2)}) collective-permute-start(bf16[544,128]{1,0:T(8,128)(2,1)} %get-tuple-element.40), channel_id=1, source_target_pairs={{0,4},{1,5},{2,6},{3,7},{4,0},{5,1},{6,2},{7,3},{8,12},{9,13},{10,... | collective-permute-start | bytes 417800 | tf_op jit(solution)/shard_map/ppermute | solution.py:37
  16.6 7.7 %collective-permute-start.3 = (bf16[544,128]{1,0:T(8,128)(2,1)}, bf16[544,128]{1,0:T(8,128)(2,1)S(1)}, u32[]{:S(2)}, u32[]{:S(2)}) collective-permute-start(bf16[544,128]{1,0:T(8,128)(2,1)} %get-tuple-element.44), channel_id=1, source_target_pairs={{0,8},{1,9},{2,10},{3,11},{4,12},{5,13},{6,14},{7,15},{8,16},{9,17... | collective-permute-start | bytes 417800 | tf_op jit(solution)/shard_map/ppermute | solution.py:37
  18.5 8.0 %collective-permute-start.4 = (bf16[544,128]{1,0:T(8,128)(2,1)}, bf16[544,128]{1,0:T(8,128)(2,1)S(1)}, u32[]{:S(2)}, u32[]{:S(2)}) collective-permute-start(bf16[544,128]{1,0:T(8,128)(2,1)} %get-tuple-element.44), channel_id=1, source_target_pairs={{0,24},{1,25},{2,26},{3,27},{4,28},{5,29},{6,30},{7,31},{8,0},{9,1... | collective-permute-start | bytes 417800 | tf_op jit(solution)/shard_map/ppermute | solution.py:37
  20.6 7.5 %collective-permute-start.5 = (bf16[544,128]{1,0:T(8,128)(2,1)}, bf16[544,128]{1,0:T(8,128)(2,1)S(1)}, u32[]{:S(2)}, u32[]{:S(2)}) collective-permute-start(bf16[544,128]{1,0:T(8,128)(2,1)} %get-tuple-element.44), channel_id=1, source_target_pairs={{0,16},{1,17},{2,18},{3,19},{4,20},{5,21},{6,22},{7,23},{8,24},{9,... | collective-permute-start | bytes 417800 | tf_op jit(solution)/shard_map/ppermute | solution.py:37
  29.1 17.4 %collective-permute-start.7 = (bf16[4,544,128]{2,1,0:T(8,128)(2,1)S(1)}, bf16[4,544,128]{2,1,0:T(8,128)(2,1)S(1)}, u32[]{:S(2)}, u32[]{:S(2)}) collective-permute-start(bf16[4,544,128]{2,1,0:T(8,128)(2,1)S(1)} %pad_maximum_fusion.1.refs_2_), channel_id=1, source_target_pairs={{0,2},{1,3},{2,4},{3,5},{4,6},{5,7},{6,0},{7,1},{8,10},{9,11},{10,... | collective-permute-start | bytes 1671176 | tf_op jit(solution)/shard_map/ppermute | solution.py:37
  29.9 16.6 %collective-permute-start.9 = (bf16[4,544,128]{2,1,0:T(8,128)(2,1)S(1)}, bf16[4,544,128]{2,1,0:T(8,128)(2,1)S(1)}, u32[]{:S(2)}, u32[]{:S(2)}) collective-permute-start(bf16[4,544,128]{2,1,0:T(8,128)(2,1)S(1)} %pad_maximum_fusion.1.refs_2_), channel_id=1, source_target_pairs={{0,6},{1,7},{2,0},{3,1},{4,2},{5,3},{6,4},{7,5},{8,14},{9,15},{10,... | collective-permute-start | bytes 1671176 | tf_op jit(solution)/shard_map/ppermute | solution.py:37
  33.4 13.4 %collective-permute-start.6 = (bf16[4,544,128]{2,1,0:T(8,128)(2,1)S(1)}, bf16[4,544,128]{2,1,0:T(8,128)(2,1)S(1)}, u32[]{:S(2)}, u32[]{:S(2)}) collective-permute-start(bf16[4,544,128]{2,1,0:T(8,128)(2,1)S(1)} %pad_maximum_fusion.refs_1_), channel_id=1, source_target_pairs={{0,8},{1,9},{2,10},{3,11},{4,12},{5,13},{6,14},{7,15},{8,16},{9,17... | collective-permute-start | bytes 1671176 | tf_op jit(solution)/shard_map/ppermute | solution.py:37
  34.3 12.5 %collective-permute-start.8 = (bf16[4,544,128]{2,1,0:T(8,128)(2,1)S(1)}, bf16[4,544,128]{2,1,0:T(8,128)(2,1)S(1)}, u32[]{:S(2)}, u32[]{:S(2)}) collective-permute-start(bf16[4,544,128]{2,1,0:T(8,128)(2,1)S(1)} %pad_maximum_fusion.refs_1_), channel_id=1, source_target_pairs={{0,24},{1,25},{2,26},{3,27},{4,28},{5,29},{6,30},{7,31},{8,0},{9,1... | collective-permute-start | bytes 1671176 | tf_op jit(solution)/shard_map/ppermute | solution.py:37
  36.8 1.2 %copy-start = (bf16[4096,128]{1,0:T(8,128)(2,1)S(1)}, bf16[4096,128]{1,0:T(8,128)(2,1)}, u32[]{:S(2)}) copy-start(bf16[4096,128]{1,0:T(8,128)(2,1)} %all-gather.3.cloned.1.call-done) | copy-start | bytes 3145732
  38.0 15.1 %copy-start.1 = (bf16[4096,128]{1,0:T(8,128)(2,1)S(1)}, bf16[4096,128]{1,0:T(8,128)(2,1)}, u32[]{:S(2)}) copy-start(bf16[4096,128]{1,0:T(8,128)(2,1)} %all-gather.3.cloned.1.call-done) | copy-start | bytes 3145732
  46.9 18.2 %collective-permute-start.10 = (bf16[4,544,128]{2,1,0:T(8,128)(2,1)S(1)}, bf16[4,544,128]{2,1,0:T(8,128)(2,1)S(1)}, u32[]{:S(2)}, u32[]{:S(2)}) collective-permute-start(bf16[4,544,128]{2,1,0:T(8,128)(2,1)S(1)} %pad_maximum_fusion.refs_1_), channel_id=1, source_target_pairs={{0,16},{1,17},{2,18},{3,19},{4,20},{5,21},{6,22},{7,23},{8,24},{9,... | collective-permute-start | bytes 1671176 | tf_op jit(solution)/shard_map/ppermute | solution.py:37
  48.5 17.5 %collective-permute-start.11 = (bf16[4,544,128]{2,1,0:T(8,128)(2,1)S(1)}, bf16[4,544,128]{2,1,0:T(8,128)(2,1)S(1)}, u32[]{:S(2)}, u32[]{:S(2)}) collective-permute-start(bf16[4,544,128]{2,1,0:T(8,128)(2,1)S(1)} %pad_maximum_fusion.1.refs_2_), channel_id=1, source_target_pairs={{0,4},{1,5},{2,6},{3,7},{4,0},{5,1},{6,2},{7,3},{8,12},{9,13},{10,... | collective-permute-start | bytes 1671176 | tf_op jit(solution)/shard_map/ppermute | solution.py:37
  74.9 6.7 %collective-permute-start.14 = (f32[4,512,128]{2,1,0:T(8,128)}, f32[4,512,128]{2,1,0:T(8,128)}, u32[]{:S(2)}, u32[]{:S(2)}) collective-permute-start(f32[4,512,128]{2,1,0:T(8,128)} %get-tuple-element.67), channel_id=1, source_target_pairs={{0,1},{1,0},{2,3},{3,2},{4,5},{5,4},{6,7},{7,6},{8,9},{9,8},{10,11... | collective-permute-start | bytes 3145736 | tf_op jit(solution)/shard_map/ppermute | solution.py:37
  75.9 1.8 %collective-permute-start.12 = (f32[4,2,512]{2,1,0:T(2,128)S(1)}, f32[4,2,512]{2,1,0:T(2,128)S(1)}, u32[]{:S(2)}, u32[]{:S(2)}) collective-permute-start(f32[4,2,512]{2,1,0:T(2,128)S(1)} %select_add_fusion), channel_id=1, source_target_pairs={{0,1},{1,0},{2,3},{3,2},{4,5},{5,4},{6,7},{7,6},{8,9},{9,8},{10,11... | collective-permute-start | bytes 49160 | tf_op jit(solution)/shard_map/ppermute | solution.py:37
  77.8 3.8 %collective-permute-start.13 = (f32[4,2,512]{2,1,0:T(2,128)S(1)}, f32[4,2,512]{2,1,0:T(2,128)S(1)}, u32[]{:S(2)}, u32[]{:S(2)}) collective-permute-start(f32[4,2,512]{2,1,0:T(2,128)S(1)} %fusion.3), channel_id=1, source_target_pairs={{0,32},{32,0},{64,96},{96,64},{1,33},{33,1},{65,97},{97,65},{2,34}... | collective-permute-start | bytes 49160 | tf_op jit(solution)/shard_map/ppermute | solution.py:45
  82.9 6.4 %collective-permute-start.15 = (f32[4,2,512]{2,1,0:T(2,128)S(1)}, f32[4,2,512]{2,1,0:T(2,128)S(1)}, u32[]{:S(2)}, u32[]{:S(2)}) collective-permute-start(f32[4,2,512]{2,1,0:T(2,128)S(1)} %add.84), channel_id=1, source_target_pairs={{0,64},{32,96},{64,0},{96,32},{1,65},{33,97},{65,1},{97,33},{2,66}... | collective-permute-start | bytes 49160 | tf_op jit(solution)/shard_map/ppermute | solution.py:45
  84.6 14.0 %collective-permute-start.16 = (f32[512,128]{1,0:T(8,128)S(1)}, f32[512,128]{1,0:T(8,128)S(1)}, u32[]{:S(2)}, u32[]{:S(2)}) collective-permute-start(f32[512,128]{1,0:T(8,128)S(1)} %get-tuple-element.75), channel_id=1, source_target_pairs={{0,32},{32,64},{64,96},{96,0},{1,33},{33,65},{65,97},{97,1},{2,34}... | collective-permute-start | bytes 786440 | tf_op jit(solution)/shard_map/ppermute | solution.py:41
  85.2 13.5 %collective-permute-start.17 = (f32[512,128]{1,0:T(8,128)S(1)}, f32[512,128]{1,0:T(8,128)S(1)}, u32[]{:S(2)}, u32[]{:S(2)}) collective-permute-start(f32[512,128]{1,0:T(8,128)S(1)} %get-tuple-element.77), channel_id=1, source_target_pairs={{0,64},{32,96},{64,0},{96,32},{1,65},{33,97},{65,1},{97,33},{2,66}... | collective-permute-start | bytes 786440 | tf_op jit(solution)/shard_map/ppermute | solution.py:41
  87.3 11.8 %collective-permute-start.18 = (f32[512,128]{1,0:T(8,128)S(1)}, f32[512,128]{1,0:T(8,128)S(1)}, u32[]{:S(2)}, u32[]{:S(2)}) collective-permute-start(f32[512,128]{1,0:T(8,128)S(1)} %get-tuple-element.76), channel_id=1, source_target_pairs={{0,96},{32,0},{64,32},{96,64},{1,97},{33,1},{65,33},{97,65},{2,98}... | collective-permute-start | bytes 786440 | tf_op jit(solution)/shard_map/ppermute | solution.py:41
  90.6 21.9 %copy-start.2 = (bf16[1024]{0:T(1024)(128)(2,1)S(1)}, bf16[1024]{0:T(1024)(128)(2,1)}, u32[]{:S(2)}) copy-start(bf16[1024]{0:T(1024)(128)(2,1)} %param.7) | copy-start | bytes 6148
  99.1 13.3 %all-to-all-start = ((f32[16,8,128]{2,1,0:T(8,128)}), f32[16,8,128]{2,1,0:T(8,128)S(1)}, u32[]{:S(2)}, u32[]{:S(2)}) async-start(f32[16,8,128]{2,1,0:T(8,128)} %bitcast.17), calls=%async_computation | async-start | bytes 131072 | tf_op jit(solution)/shard_map/all_to_all | solution.py:424
  (1 other events, 0.9 us)
Sparse Core Ops, SparseCore 0:
  9.7 25.7 all-gather.2

commit v4 on v3

--- a/solution.py
+++ b/solution.py
@@ -131,7 +131,7 @@
                 d = det_ref[r, h:h + 128, :].astype(f32)
                 v = jnp.sum(d * d, axis=1, keepdims=True) * (-0.5 * SCALE) + 16.0 * LOG2E
                 as_ref[r, h:h + 128, :] = jnp.broadcast_to(v, (128, 128))
-    else:
+    elif last:
         mom_ref[...] = mom_in[...]
         mass_ref[...] = mass_in[...]
     base = jnp.int32(0)
@@ -277,6 +277,8 @@
         operands += tables + list(state)
         specs += [sm] * len(tables) + [vm, vm, vm, hb]
         aliases = {len(specs) - 1: 2 + last}
+        if not last:
+            aliases.update({len(specs) - 4: 0, len(specs) - 3: 1})
     if last:
         outs, out_specs = [half, half] + outs[1:], [hb, hb] + out_specs[1:]
         extra = [pltpu.VMEM((9, DBS, 128), f32), pltpu.SemaphoreType.DMA((8,))]

time: 121 us -> 121 us (level); the launches traced: 120 us -> 122 us
  starting transfers between devices: 36.8 us -> 39.2 us
    all_to_all x1, starting transfers between devices: 5.64 us -> 8.81 us  [local(): lax.all_to_all(share.reshape(16, 8, 128), 'gy', split_axis=0, concat_axis...]
  transfers between devices with their start and end apart: 21 -> 21, of which waited for: 10 -> 8; matrix products, arithmetic and copies ran while one was open for 4% -> 4% of each run, Pallas kernels for 26% -> 25%
where the time goes in v4:
time: 121 us; the launch traced here: 122 us
  Pallas kernels  39.4 us (33%)
  starting transfers between devices  39.2 us (32%)
  waiting for transfers between devices  20.2 us (17%)
  between operations  14.3 us (12%)
  other arithmetic  5.83 us (5%)
  local copies, waits for them, and re-layouts  2.53 us (2%)
    pallas_call x3, Pallas kernels, pair_call(): pl.pallas_call(functools.partial(pair_kernel, steps, len(tables), last),...  28.9 us
    ppermute x14, starting transfers between devices, gy_shift(): return lax.ppermute(v, 'gy', perm)  24 us
    all_to_all x1, starting transfers between devices, local(): lax.all_to_all(share.reshape(16, 8, 128), 'gy', split_axis=0, concat_axis...  8.81 us
    ppermute x14, waiting for transfers between devices, gy_shift(): return lax.ppermute(v, 'gy', perm)  8.46 us
    pallas_call x1, Pallas kernels, share_call(): pl.pallas_call(share_kernel, out_shape=jax.ShapeDtypeStruct((NONE, 128),...  7.12 us
    all_to_all x1, waiting for transfers between devices, local(): lax.all_to_all(share.reshape(16, 8, 128), 'gy', split_axis=0, concat_axis...  6.82 us
    ppermute x3, starting transfers between devices, x_shift(): return lax.ppermute(v, 'gx', [(i, (i + s) % 4) for i in range(4)])  5.54 us
    ppermute x2, waiting for transfers between devices, x_swap(): return lax.ppermute(v, 'gx', [(i, i ^ s) for i in range(4)])  3.68 us
  transfers between devices with their start and end apart: 21, of which 8 were waited for; matrix products, arithmetic and copies ran while one was open for 4% of the time, Pallas kernels for 25%

profile of v4, /device:TPU:0, one launch (start us, length us, event | category | flops | bytes accessed | tf_op | source)
XLA Modules:
  0.0 121.5 jit_solution(14155302689468405625)
XLA Ops:
  7.9 3.4 %payload.1 = (bf16[544,128]{1,0:T(8,128)(2,1)}, bf16[544,128]{1,0:T(8,128)(2,1)}) custom-call(s32[8,16]{1,0:T(8,128)} %ids_ref.1, s32[8]{0:T(128)} %lens_ref.1, bf16[1024,128]{1,0:T(8,128)(2,1)} %part_ref.1, bf16[8,128]{1,0:T(8,128)(2,1)} %bitcast.42), custom_call_target="tpu_custom_call" | custom-call | tf_op jit(solution)/shard_map/payload/pallas_call | solution.py:83
  11.3 1.7 %collective-permute-start = (bf16[544,128]{1,0:T(8,128)(2,1)}, bf16[544,128]{1,0:T(8,128)(2,1)S(1)}, u32[]{:S(2)}, u32[]{:S(2)}) collective-permute-start(bf16[544,128]{1,0:T(8,128)(2,1)} %get-tuple-element.40), channel_id=1, source_target_pairs={{0,2},{1,3},{2,4},{3,5},{4,6},{5,7},{6,0},{7,1},{8,10},{9,11},{10,... | collective-permute-start | bytes 417800 | tf_op jit(solution)/shard_map/ppermute | solution.py:37
  12.9 1.6 %collective-permute-start.1 = (bf16[544,128]{1,0:T(8,128)(2,1)}, bf16[544,128]{1,0:T(8,128)(2,1)S(1)}, u32[]{:S(2)}, u32[]{:S(2)}) collective-permute-start(bf16[544,128]{1,0:T(8,128)(2,1)} %get-tuple-element.40), channel_id=1, source_target_pairs={{0,6},{1,7},{2,0},{3,1},{4,2},{5,3},{6,4},{7,5},{8,14},{9,15},{10,... | collective-permute-start | bytes 417800 | tf_op jit(solution)/shard_map/ppermute | solution.py:37
  14.5 2.1 %collective-permute-start.2 = (bf16[544,128]{1,0:T(8,128)(2,1)}, bf16[544,128]{1,0:T(8,128)(2,1)S(1)}, u32[]{:S(2)}, u32[]{:S(2)}) collective-permute-start(bf16[544,128]{1,0:T(8,128)(2,1)} %get-tuple-element.40), channel_id=1, source_target_pairs={{0,4},{1,5},{2,6},{3,7},{4,0},{5,1},{6,2},{7,3},{8,12},{9,13},{10,... | collective-permute-start | bytes 417800 | tf_op jit(solution)/shard_map/ppermute | solution.py:37
  16.6 1.9 %collective-permute-start.3 = (bf16[544,128]{1,0:T(8,128)(2,1)}, bf16[544,128]{1,0:T(8,128)(2,1)S(1)}, u32[]{:S(2)}, u32[]{:S(2)}) collective-permute-start(bf16[544,128]{1,0:T(8,128)(2,1)} %get-tuple-element.44), channel_id=1, source_target_pairs={{0,8},{1,9},{2,10},{3,11},{4,12},{5,13},{6,14},{7,15},{8,16},{9,17... | collective-permute-start | bytes 417800 | tf_op jit(solution)/shard_map/ppermute | solution.py:37
  18.5 2.1 %collective-permute-start.4 = (bf16[544,128]{1,0:T(8,128)(2,1)}, bf16[544,128]{1,0:T(8,128)(2,1)S(1)}, u32[]{:S(2)}, u32[]{:S(2)}) collective-permute-start(bf16[544,128]{1,0:T(8,128)(2,1)} %get-tuple-element.44), channel_id=1, source_target_pairs={{0,24},{1,25},{2,26},{3,27},{4,28},{5,29},{6,30},{7,31},{8,0},{9,1... | collective-permute-start | bytes 417800 | tf_op jit(solution)/shard_map/ppermute | solution.py:37
  20.6 1.9 %collective-permute-start.5 = (bf16[544,128]{1,0:T(8,128)(2,1)}, bf16[544,128]{1,0:T(8,128)(2,1)S(1)}, u32[]{:S(2)}, u32[]{:S(2)}) collective-permute-start(bf16[544,128]{1,0:T(8,128)(2,1)} %get-tuple-element.44), channel_id=1, source_target_pairs={{0,16},{1,17},{2,18},{3,19},{4,20},{5,21},{6,22},{7,23},{8,24},{9,... | collective-permute-start | bytes 417800 | tf_op jit(solution)/shard_map/ppermute | solution.py:37
  22.5 1.8 %collective-permute-done.3 = bf16[544,128]{1,0:T(8,128)(2,1)S(1)} collective-permute-done((bf16[544,128]{1,0:T(8,128)(2,1)}, bf16[544,128]{1,0:T(8,128)(2,1)S(1)}, u32[]{:S(2)}, u32[]{:S(2)}) %collective-permute-start.3) | collective-permute-done | bytes 139296 | tf_op jit(solution)/shard_map/ppermute | solution.py:37
  24.2 2.3 %collective-permute-done.4 = bf16[544,128]{1,0:T(8,128)(2,1)S(1)} collective-permute-done((bf16[544,128]{1,0:T(8,128)(2,1)}, bf16[544,128]{1,0:T(8,128)(2,1)S(1)}, u32[]{:S(2)}, u32[]{:S(2)}) %collective-permute-start.4) | collective-permute-done | bytes 139296 | tf_op jit(solution)/shard_map/ppermute | solution.py:37
  26.5 1.6 %collective-permute-done.5 = bf16[544,128]{1,0:T(8,128)(2,1)S(1)} collective-permute-done((bf16[544,128]{1,0:T(8,128)(2,1)}, bf16[544,128]{1,0:T(8,128)(2,1)S(1)}, u32[]{:S(2)}, u32[]{:S(2)}) %collective-permute-start.5) | collective-permute-done | bytes 139296 | tf_op jit(solution)/shard_map/ppermute | solution.py:37
  29.9 2.6 %collective-permute-start.9 = (bf16[4,544,128]{2,1,0:T(8,128)(2,1)S(1)}, bf16[4,544,128]{2,1,0:T(8,128)(2,1)S(1)}, u32[]{:S(2)}, u32[]{:S(2)}) collective-permute-start(bf16[4,544,128]{2,1,0:T(8,128)(2,1)S(1)} %pad_maximum_fusion.1.refs_2_), channel_id=1, source_target_pairs={{0,6},{1,7},{2,0},{3,1},{4,2},{5,3},{6,4},{7,5},{8,14},{9,15},{10,... | collective-permute-start | bytes 1671176 | tf_op jit(solution)/shard_map/ppermute | solution.py:37
  34.3 2.4 %collective-permute-start.8 = (bf16[4,544,128]{2,1,0:T(8,128)(2,1)S(1)}, bf16[4,544,128]{2,1,0:T(8,128)(2,1)S(1)}, u32[]{:S(2)}, u32[]{:S(2)}) collective-permute-start(bf16[4,544,128]{2,1,0:T(8,128)(2,1)S(1)} %pad_maximum_fusion.refs_1_), channel_id=1, source_target_pairs={{0,24},{1,25},{2,26},{3,27},{4,28},{5,29},{6,30},{7,31},{8,0},{9,1... | collective-permute-start | bytes 1671176 | tf_op jit(solution)/shard_map/ppermute | solution.py:37
  38.0 8.8 %pairs.3 = (f32[9,512,128]{2,1,0:T(8,128)S(1)}, f32[9,512,128]{2,1,0:T(8,128)S(1)}, bf16[100,2,512,256]{3,2,1,0:T(8,128)(2,1)}, s32[4,152]{1,0:T(4,128)S(1)}, f32[8,512,128]{2,1,0:T(8,128)S(1)}) custom-call(s32[3]{0:T(128)S(1)} %pad_add_fusion.refs_0_, bf16[4,544,128]{2,1,0:T(8,128)(2,1)S(1)} %pad_maximum_fusion.refs_1_, ...), custom_call_target="tpu_custom_call" | custom-call | flops 872415232 | bytes 3407872 | tf_op jit(solution)/shard_map/pairs/pallas_call | solution.py:286
  46.9 1.4 %collective-permute-start.10 = (bf16[4,544,128]{2,1,0:T(8,128)(2,1)S(1)}, bf16[4,544,128]{2,1,0:T(8,128)(2,1)S(1)}, u32[]{:S(2)}, u32[]{:S(2)}) collective-permute-start(bf16[4,544,128]{2,1,0:T(8,128)(2,1)S(1)} %pad_maximum_fusion.refs_1_), channel_id=1, source_target_pairs={{0,16},{1,17},{2,18},{3,19},{4,20},{5,21},{6,22},{7,23},{8,24},{9,... | collective-permute-start | bytes 1671176 | tf_op jit(solution)/shard_map/ppermute | solution.py:37
  48.3 4.1 %collective-permute-start.11 = (bf16[4,544,128]{2,1,0:T(8,128)(2,1)S(1)}, bf16[4,544,128]{2,1,0:T(8,128)(2,1)S(1)}, u32[]{:S(2)}, u32[]{:S(2)}) collective-permute-start(bf16[4,544,128]{2,1,0:T(8,128)(2,1)S(1)} %pad_maximum_fusion.1.refs_2_), channel_id=1, source_target_pairs={{0,4},{1,5},{2,6},{3,7},{4,0},{5,1},{6,2},{7,3},{8,12},{9,13},{10,... | collective-permute-start | bytes 1671176 | tf_op jit(solution)/shard_map/ppermute | solution.py:37
  52.5 11.2 %pairs.4 = (f32[9,512,128]{2,1,0:T(8,128)S(1)}, f32[9,512,128]{2,1,0:T(8,128)S(1)}, bf16[100,2,512,256]{3,2,1,0:T(8,128)(2,1)}, s32[4,152]{1,0:T(4,128)S(1)}) custom-call(s32[3]{0:T(128)S(1)} %pad_add_fusion.refs_0_, bf16[4,544,128]{2,1,0:T(8,128)(2,1)S(1)} %collective-permute-done.6.refs_1_, ...), custom_call_target="tpu_custom_call", output_to_operand_aliasing={{2}: (10, {}), {0}: (7, {}), {1}: (8, {})} | custom-call | flops 1744830464 | bytes 6815744 | tf_op jit(solution)/shard_map/pairs/pallas_call | solution.py:286
  63.7 1.6 %collective-permute-done.11.refs_2_ = bf16[4,544,128]{2,1,0:T(8,128)(2,1)S(1)} collective-permute-done((bf16[4,544,128]{2,1,0:T(8,128)(2,1)S(1)}, bf16[4,544,128]{2,1,0:T(8,128)(2,1)S(1)}, u32[]{:S(2)}, u32[]{:S(2)}) %collective-permute-start.11) | collective-permute-done | bytes 557088 | tf_op jit(solution)/shard_map/ppermute | solution.py:37
  65.2 8.9 %pairs.5 = (f32[4,512,128]{2,1,0:T(8,128)S(1)}, f32[4,512,128]{2,1,0:T(8,128)}, f32[9,512,128]{2,1,0:T(8,128)S(1)}, bf16[100,2,512,256]{3,2,1,0:T(8,128)(2,1)}, s32[4,152]{1,0:T(4,128)S(1)}) custom-call(s32[3]{0:T(128)S(1)} %pad_add_fusion.refs_0_, bf16[4,544,128]{2,1,0:T(8,128)(2,1)S(1)} %collective-permute-done.10.refs_1_, ...), custom_call_target="tpu_custom_call", output_to_operand_aliasing={{3}: (9, {})} | custom-call | flops 872415232 | bytes 3407872 | tf_op jit(solution)/shard_map/pairs/pallas_call | solution.py:286
  77.2 3.7 %collective-permute-done.13 = f32[4,2,512]{2,1,0:T(2,128)S(1)} collective-permute-done((f32[4,2,512]{2,1,0:T(2,128)S(1)}, f32[4,2,512]{2,1,0:T(2,128)S(1)}, u32[]{:S(2)}, u32[]{:S(2)}) %collective-permute-start.13) | collective-permute-done | bytes 16416 | tf_op jit(solution)/shard_map/ppermute | solution.py:45
  83.4 3.2 %collective-permute-start.17 = (f32[512,128]{1,0:T(8,128)S(1)}, f32[512,128]{1,0:T(8,128)S(1)}, u32[]{:S(2)}, u32[]{:S(2)}) collective-permute-start(f32[512,128]{1,0:T(8,128)S(1)} %get-tuple-element.77), channel_id=1, source_target_pairs={{0,64},{32,96},{64,0},{96,32},{1,65},{33,97},{65,1},{97,33},{2,66}... | collective-permute-start | bytes 786440 | tf_op jit(solution)/shard_map/ppermute | solution.py:41
  86.5 2.0 %collective-permute-start.18 = (f32[512,128]{1,0:T(8,128)S(1)}, f32[512,128]{1,0:T(8,128)S(1)}, u32[]{:S(2)}, u32[]{:S(2)}) collective-permute-start(f32[512,128]{1,0:T(8,128)S(1)} %get-tuple-element.76), channel_id=1, source_target_pairs={{0,96},{32,0},{64,32},{96,64},{1,97},{33,1},{65,33},{97,65},{2,98}... | collective-permute-start | bytes 786440 | tf_op jit(solution)/shard_map/ppermute | solution.py:41
  89.8 7.1 %shares.1 = f32[128,128]{1,0:T(8,128)} custom-call(s32[4,152]{1,0:T(4,128)S(1)} %get-tuple-element.49.refs_6_.refs_4_.ta, s32[4,152]{1,0:T(4,128)S(1)} %get-tuple-element.58.refs_5_.tb, s32[4,152]{1,0:T(4,128)S(1)} %get-tuple-element.64.tc, f32[8,512,128]{2,1,0:T(8,128)S(1)} %broadcast_in_dim.39.inv_ref, bf16[100,2,512,256]{3,2,1,0:T(8,128)(2,1)} %get-tuple-element.69.low_ref), custom_call_target="tpu_custom_call" | custom-call | flops 13631488 | bytes 13631488 | tf_op jit(solution)/shard_map/shares/pallas_call | solution.py:369
  97.6 8.8 %all-to-all-start = ((f32[16,8,128]{2,1,0:T(8,128)}), f32[16,8,128]{2,1,0:T(8,128)S(1)}, u32[]{:S(2)}, u32[]{:S(2)}) async-start(f32[16,8,128]{2,1,0:T(8,128)} %bitcast.17), calls=%async_computation | async-start | bytes 131072 | tf_op jit(solution)/shard_map/all_to_all | solution.py:426
  107.2 6.8 %all-to-all-done = f32[16,8,128]{2,1,0:T(8,128)S(1)} async-done(((f32[16,8,128]{2,1,0:T(8,128)}), f32[16,8,128]{2,1,0:T(8,128)S(1)}, u32[]{:S(2)}, u32[]{:S(2)}) %all-to-all-start) | async-done | bytes 65568 | tf_op jit(solution)/shard_map/all_to_all | solution.py:426
  (54 shorter events, 14.4 us)
Async XLA Ops:
  7.2 29.6 %all-gather.3.cloned.1.call-start = ((), (), s32[]{:S(2)}) async-start(), calls=%async_computation.1 | async-start | bytes 1179648 | tf_op jit(solution)/shard_map/all_gather | solution.py:391
  11.3 9.3 %collective-permute-start = (bf16[544,128]{1,0:T(8,128)(2,1)}, bf16[544,128]{1,0:T(8,128)(2,1)S(1)}, u32[]{:S(2)}, u32[]{:S(2)}) collective-permute-start(bf16[544,128]{1,0:T(8,128)(2,1)} %get-tuple-element.40), channel_id=1, source_target_pairs={{0,2},{1,3},{2,4},{3,5},{4,6},{5,7},{6,0},{7,1},{8,10},{9,11},{10,... | collective-permute-start | bytes 417800 | tf_op jit(solution)/shard_map/ppermute | solution.py:37
  12.9 9.6 %collective-permute-start.1 = (bf16[544,128]{1,0:T(8,128)(2,1)}, bf16[544,128]{1,0:T(8,128)(2,1)S(1)}, u32[]{:S(2)}, u32[]{:S(2)}) collective-permute-start(bf16[544,128]{1,0:T(8,128)(2,1)} %get-tuple-element.40), channel_id=1, source_target_pairs={{0,6},{1,7},{2,0},{3,1},{4,2},{5,3},{6,4},{7,5},{8,14},{9,15},{10,... | collective-permute-start | bytes 417800 | tf_op jit(solution)/shard_map/ppermute | solution.py:37
  14.5 8.0 %collective-permute-start.2 = (bf16[544,128]{1,0:T(8,128)(2,1)}, bf16[544,128]{1,0:T(8,128)(2,1)S(1)}, u32[]{:S(2)}, u32[]{:S(2)}) collective-permute-start(bf16[544,128]{1,0:T(8,128)(2,1)} %get-tuple-element.40), channel_id=1, source_target_pairs={{0,4},{1,5},{2,6},{3,7},{4,0},{5,1},{6,2},{7,3},{8,12},{9,13},{10,... | collective-permute-start | bytes 417800 | tf_op jit(solution)/shard_map/ppermute | solution.py:37
  16.6 7.7 %collective-permute-start.3 = (bf16[544,128]{1,0:T(8,128)(2,1)}, bf16[544,128]{1,0:T(8,128)(2,1)S(1)}, u32[]{:S(2)}, u32[]{:S(2)}) collective-permute-start(bf16[544,128]{1,0:T(8,128)(2,1)} %get-tuple-element.44), channel_id=1, source_target_pairs={{0,8},{1,9},{2,10},{3,11},{4,12},{5,13},{6,14},{7,15},{8,16},{9,17... | collective-permute-start | bytes 417800 | tf_op jit(solution)/shard_map/ppermute | solution.py:37
  18.5 8.0 %collective-permute-start.4 = (bf16[544,128]{1,0:T(8,128)(2,1)}, bf16[544,128]{1,0:T(8,128)(2,1)S(1)}, u32[]{:S(2)}, u32[]{:S(2)}) collective-permute-start(bf16[544,128]{1,0:T(8,128)(2,1)} %get-tuple-element.44), channel_id=1, source_target_pairs={{0,24},{1,25},{2,26},{3,27},{4,28},{5,29},{6,30},{7,31},{8,0},{9,1... | collective-permute-start | bytes 417800 | tf_op jit(solution)/shard_map/ppermute | solution.py:37
  20.6 7.5 %collective-permute-start.5 = (bf16[544,128]{1,0:T(8,128)(2,1)}, bf16[544,128]{1,0:T(8,128)(2,1)S(1)}, u32[]{:S(2)}, u32[]{:S(2)}) collective-permute-start(bf16[544,128]{1,0:T(8,128)(2,1)} %get-tuple-element.44), channel_id=1, source_target_pairs={{0,16},{1,17},{2,18},{3,19},{4,20},{5,21},{6,22},{7,23},{8,24},{9,... | collective-permute-start | bytes 417800 | tf_op jit(solution)/shard_map/ppermute | solution.py:37
  29.1 17.8 %collective-permute-start.7 = (bf16[4,544,128]{2,1,0:T(8,128)(2,1)S(1)}, bf16[4,544,128]{2,1,0:T(8,128)(2,1)S(1)}, u32[]{:S(2)}, u32[]{:S(2)}) collective-permute-start(bf16[4,544,128]{2,1,0:T(8,128)(2,1)S(1)} %pad_maximum_fusion.1.refs_2_), channel_id=1, source_target_pairs={{0,2},{1,3},{2,4},{3,5},{4,6},{5,7},{6,0},{7,1},{8,10},{9,11},{10,... | collective-permute-start | bytes 1671176 | tf_op jit(solution)/shard_map/ppermute | solution.py:37
  29.9 17.0 %collective-permute-start.9 = (bf16[4,544,128]{2,1,0:T(8,128)(2,1)S(1)}, bf16[4,544,128]{2,1,0:T(8,128)(2,1)S(1)}, u32[]{:S(2)}, u32[]{:S(2)}) collective-permute-start(bf16[4,544,128]{2,1,0:T(8,128)(2,1)S(1)} %pad_maximum_fusion.1.refs_2_), channel_id=1, source_target_pairs={{0,6},{1,7},{2,0},{3,1},{4,2},{5,3},{6,4},{7,5},{8,14},{9,15},{10,... | collective-permute-start | bytes 1671176 | tf_op jit(solution)/shard_map/ppermute | solution.py:37
  33.4 13.5 %collective-permute-start.6 = (bf16[4,544,128]{2,1,0:T(8,128)(2,1)S(1)}, bf16[4,544,128]{2,1,0:T(8,128)(2,1)S(1)}, u32[]{:S(2)}, u32[]{:S(2)}) collective-permute-start(bf16[4,544,128]{2,1,0:T(8,128)(2,1)S(1)} %pad_maximum_fusion.refs_1_), channel_id=1, source_target_pairs={{0,8},{1,9},{2,10},{3,11},{4,12},{5,13},{6,14},{7,15},{8,16},{9,17... | collective-permute-start | bytes 1671176 | tf_op jit(solution)/shard_map/ppermute | solution.py:37
  34.3 12.6 %collective-permute-start.8 = (bf16[4,544,128]{2,1,0:T(8,128)(2,1)S(1)}, bf16[4,544,128]{2,1,0:T(8,128)(2,1)S(1)}, u32[]{:S(2)}, u32[]{:S(2)}) collective-permute-start(bf16[4,544,128]{2,1,0:T(8,128)(2,1)S(1)} %pad_maximum_fusion.refs_1_), channel_id=1, source_target_pairs={{0,24},{1,25},{2,26},{3,27},{4,28},{5,29},{6,30},{7,31},{8,0},{9,1... | collective-permute-start | bytes 1671176 | tf_op jit(solution)/shard_map/ppermute | solution.py:37
  36.8 1.2 %copy-start = (bf16[4096,128]{1,0:T(8,128)(2,1)S(1)}, bf16[4096,128]{1,0:T(8,128)(2,1)}, u32[]{:S(2)}) copy-start(bf16[4096,128]{1,0:T(8,128)(2,1)} %all-gather.3.cloned.1.call-done) | copy-start | bytes 3145732
  46.9 16.7 %collective-permute-start.10 = (bf16[4,544,128]{2,1,0:T(8,128)(2,1)S(1)}, bf16[4,544,128]{2,1,0:T(8,128)(2,1)S(1)}, u32[]{:S(2)}, u32[]{:S(2)}) collective-permute-start(bf16[4,544,128]{2,1,0:T(8,128)(2,1)S(1)} %pad_maximum_fusion.refs_1_), channel_id=1, source_target_pairs={{0,16},{1,17},{2,18},{3,19},{4,20},{5,21},{6,22},{7,23},{8,24},{9,... | collective-permute-start | bytes 1671176 | tf_op jit(solution)/shard_map/ppermute | solution.py:37
  48.3 16.9 %collective-permute-start.11 = (bf16[4,544,128]{2,1,0:T(8,128)(2,1)S(1)}, bf16[4,544,128]{2,1,0:T(8,128)(2,1)S(1)}, u32[]{:S(2)}, u32[]{:S(2)}) collective-permute-start(bf16[4,544,128]{2,1,0:T(8,128)(2,1)S(1)} %pad_maximum_fusion.1.refs_2_), channel_id=1, source_target_pairs={{0,4},{1,5},{2,6},{3,7},{4,0},{5,1},{6,2},{7,3},{8,12},{9,13},{10,... | collective-permute-start | bytes 1671176 | tf_op jit(solution)/shard_map/ppermute | solution.py:37
  74.2 1.0 copy-start.2
  74.2 6.7 %collective-permute-start.14 = (f32[4,512,128]{2,1,0:T(8,128)}, f32[4,512,128]{2,1,0:T(8,128)}, u32[]{:S(2)}, u32[]{:S(2)}) collective-permute-start(f32[4,512,128]{2,1,0:T(8,128)} %get-tuple-element.67), channel_id=1, source_target_pairs={{0,1},{1,0},{2,3},{3,2},{4,5},{5,4},{6,7},{7,6},{8,9},{9,8},{10,11... | collective-permute-start | bytes 3145736 | tf_op jit(solution)/shard_map/ppermute | solution.py:37
  75.2 1.7 %collective-permute-start.12 = (f32[4,2,512]{2,1,0:T(2,128)S(1)}, f32[4,2,512]{2,1,0:T(2,128)S(1)}, u32[]{:S(2)}, u32[]{:S(2)}) collective-permute-start(f32[4,2,512]{2,1,0:T(2,128)S(1)} %select_add_fusion), channel_id=1, source_target_pairs={{0,1},{1,0},{2,3},{3,2},{4,5},{5,4},{6,7},{7,6},{8,9},{9,8},{10,11... | collective-permute-start | bytes 49160 | tf_op jit(solution)/shard_map/ppermute | solution.py:37
  77.0 3.8 %collective-permute-start.13 = (f32[4,2,512]{2,1,0:T(2,128)S(1)}, f32[4,2,512]{2,1,0:T(2,128)S(1)}, u32[]{:S(2)}, u32[]{:S(2)}) collective-permute-start(f32[4,2,512]{2,1,0:T(2,128)S(1)} %fusion.3), channel_id=1, source_target_pairs={{0,32},{32,0},{64,96},{96,64},{1,33},{33,1},{65,97},{97,65},{2,34}... | collective-permute-start | bytes 49160 | tf_op jit(solution)/shard_map/ppermute | solution.py:45
  82.2 6.4 %collective-permute-start.15 = (f32[4,2,512]{2,1,0:T(2,128)S(1)}, f32[4,2,512]{2,1,0:T(2,128)S(1)}, u32[]{:S(2)}, u32[]{:S(2)}) collective-permute-start(f32[4,2,512]{2,1,0:T(2,128)S(1)} %add.84), channel_id=1, source_target_pairs={{0,64},{32,96},{64,0},{96,32},{1,65},{33,97},{65,1},{97,33},{2,66}... | collective-permute-start | bytes 49160 | tf_op jit(solution)/shard_map/ppermute | solution.py:45
  83.0 14.0 %collective-permute-start.16 = (f32[512,128]{1,0:T(8,128)S(1)}, f32[512,128]{1,0:T(8,128)S(1)}, u32[]{:S(2)}, u32[]{:S(2)}) collective-permute-start(f32[512,128]{1,0:T(8,128)S(1)} %get-tuple-element.75), channel_id=1, source_target_pairs={{0,32},{32,64},{64,96},{96,0},{1,33},{33,65},{65,97},{97,1},{2,34}... | collective-permute-start | bytes 786440 | tf_op jit(solution)/shard_map/ppermute | solution.py:41
  83.4 14.1 %collective-permute-start.17 = (f32[512,128]{1,0:T(8,128)S(1)}, f32[512,128]{1,0:T(8,128)S(1)}, u32[]{:S(2)}, u32[]{:S(2)}) collective-permute-start(f32[512,128]{1,0:T(8,128)S(1)} %get-tuple-element.77), channel_id=1, source_target_pairs={{0,64},{32,96},{64,0},{96,32},{1,65},{33,97},{65,1},{97,33},{2,66}... | collective-permute-start | bytes 786440 | tf_op jit(solution)/shard_map/ppermute | solution.py:41
  86.5 11.0 %collective-permute-start.18 = (f32[512,128]{1,0:T(8,128)S(1)}, f32[512,128]{1,0:T(8,128)S(1)}, u32[]{:S(2)}, u32[]{:S(2)}) collective-permute-start(f32[512,128]{1,0:T(8,128)S(1)} %get-tuple-element.76), channel_id=1, source_target_pairs={{0,96},{32,0},{64,32},{96,64},{1,97},{33,1},{65,33},{97,65},{2,98}... | collective-permute-start | bytes 786440 | tf_op jit(solution)/shard_map/ppermute | solution.py:41
  89.8 24.2 %copy-start.1 = (bf16[1024]{0:T(1024)(128)(2,1)S(1)}, bf16[1024]{0:T(1024)(128)(2,1)}, u32[]{:S(2)}) copy-start(bf16[1024]{0:T(1024)(128)(2,1)} %param.7) | copy-start | bytes 6148
  97.6 16.5 %all-to-all-start = ((f32[16,8,128]{2,1,0:T(8,128)}), f32[16,8,128]{2,1,0:T(8,128)S(1)}, u32[]{:S(2)}, u32[]{:S(2)}) async-start(f32[16,8,128]{2,1,0:T(8,128)} %bitcast.17), calls=%async_computation | async-start | bytes 131072 | tf_op jit(solution)/shard_map/all_to_all | solution.py:426
Sparse Core Ops, SparseCore 0:
  9.7 25.7 all-gather.2
